TPU v7x, 32 devices: a whole 2x2x4 slice. The times are simulated.
32 devices in a mesh: feat: 8 (over z, y), layer: 4 (over x, core).
Axes of the slice: x: 2, y: 2, z: 4, core: 2. Of those that a mesh axis runs over, the one named last changes fastest.
Arguments:
- resid_in: bfloat16 [4, 512, 2304], P('layer', 'feat'), may hold values from -6 to 6
- enc_weight: bfloat16 [4, 2304, 4096], P('layer', None, 'feat'), may hold values from -0.125 to 0.125
- enc_bias: float32 [4, 4096], P('layer', 'feat'), may hold values from -3 to 3
- dec_weight: bfloat16 [4, 4, 4096, 2304], P('layer', None, 'feat'), may hold values from -0.09375 to 0.09375
- dec_bias: float32 [4, 2304], P('layer'), may hold values from -3 to 3
Outputs:
- recon: bfloat16 [4, 512, 2304], P('layer', 'feat')
All inputs are finite; a program needn't handle non-finite values.
Results may differ from a plain program's by a relative error of at most 0.0046.
Values may be sent and summed in bfloat16 or wider, within the bound.
No kernel may reach another device: no remote copies, remote signals or barrier semaphores. Data moves between devices by JAX's collectives and lax.ppermute only.
A program may use at most 128 MiB of HBM per device.

v0:
```python
import jax
import jax.numpy as jnp
from jax import lax
from jax.sharding import PartitionSpec as P


def per_device(resid_in, enc_weight, enc_bias, dec_weight, dec_bias):
    preact = (
        jnp.dot(
            lax.all_gather(resid_in, "feat", axis=1, tiled=True)[0],
            enc_weight[0],
            preferred_element_type=jnp.float32,
        )
        + enc_bias[0][None, :]
    )
    actives = jnp.maximum(preact, 0.0).astype(jnp.bfloat16)[None]
    source = lax.axis_index("layer")
    total_rows = actives.shape[1]
    model_width = dec_weight.shape[3]
    incoming = lax.all_to_all(dec_weight, "layer", split_axis=1, concat_axis=0, tiled=True)
    every_actives = lax.all_gather(actives, "layer", axis=0, tiled=True)

    def accumulate(earlier, running):
        weight = lax.dynamic_index_in_dim(incoming, earlier, 0, keepdims=False)[0]
        rows = lax.dynamic_index_in_dim(every_actives, earlier, 0, keepdims=False)
        return running + jnp.dot(rows, weight, preferred_element_type=jnp.float32)

    start_sum = jnp.zeros((total_rows, model_width), jnp.float32)
    own_sum = lax.fori_loop(0, source + 1, accumulate, start_sum)
    summed = lax.psum_scatter(own_sum[None], "feat", scatter_dimension=1, tiled=True)
    return (summed + dec_bias[:, None, :]).astype(jnp.bfloat16)


def solution(mesh):
    return jax.shard_map(
        per_device,
        mesh=mesh,
        in_specs=(
            P("layer", "feat", None),
            P("layer", None, "feat"),
            P("layer", "feat"),
            P("layer", None, "feat", None),
            P("layer", None),
        ),
        out_specs=P("layer", "feat", None),
        check_vma=False,
    )
```

profile of v0, /device:TPU:0, one launch (start us, length us, event | category | flops | bytes accessed | tf_op | source)
XLA Modules:
  0.0 263.9 jit_solution(3866736947487515531)
XLA Ops:
  6.5 0.0 copy-start
  6.5 0.0 all-gather.4.cloned.1.call-start
  6.5 0.7 all-gather.4.cloned.1.call-update
  7.3 0.0 copy-start.2
  7.3 5.8 %all-to-all-start = ((bf16[1,4,512,2304]{3,2,0,1:T(8,128)(2,1)}), bf16[1,4,512,2304]{3,2,0,1:T(8,128)(2,1)}, u32[]{:S(2)}, u32[]{:S(2)}) async-start(bf16[1,4,512,2304]{3,2,0,1:T(8,128)(2,1)} %bitcast.36), calls=%async_computation | async-start | bytes 18874368 | tf_op jit(solution)/shard_map/all_to_all | solution.py:20
  13.1 0.0 all-gather.6.cloned.1.call-start
  13.1 50.8 %all-gather.4.cloned.1.call-done = bf16[1,512,2304]{2,1,0:T(8,128)(2,1)} async-done(((bf16[1,64,2304]{2,1,0:T(8,128)(2,1)}), bf16[1,512,2304]{2,1,0:T(8,128)(2,1)}) %all-gather.4.cloned.1.call-update) | async-done | bytes 2359312 | tf_op jit(solution)/shard_map/all_gather | solution.py:10
  63.9 0.0 copy-done
  63.9 0.0 copy-done.2
  63.9 3.8 %fusion.18 = bf16[512,512]{1,0:T(8,128)(2,1)} fusion(bf16[1,2304,512]{2,1,0:T(8,128)(2,1)S(1)} %copy-done, bf16[1,512,2304]{2,1,0:T(8,128)(2,1)} %all-gather.4.cloned.1.call-done, f32[512]{0:T(512)S(1)} %bitcast.38), kind=kOutput, calls=%fused_computation.11 | convolution fusion | flops 1208745984 | bytes 5244928 | tf_op jit(solution)/shard_map/dot_general | solution.py:9
  67.7 0.0 all-gather.6.cloned.1.call-update
  67.8 0.0 reduce-scatter.2.cloned.1.call-start
  67.8 61.6 %all-to-all-done = bf16[1,4,512,2304]{3,2,0,1:T(8,128)(2,1)} async-done(((bf16[1,4,512,2304]{3,2,0,1:T(8,128)(2,1)}), bf16[1,4,512,2304]{3,2,0,1:T(8,128)(2,1)}, u32[]{:S(2)}, u32[]{:S(2)}) %all-to-all-start) | async-done | bytes 9437216 | tf_op jit(solution)/shard_map/all_to_all | solution.py:20
  129.4 0.0 all-gather.6.cloned.1.call-done
  129.4 2.5 broadcast_in_dim.10
  132.0 6.8 %while.10 = (s32[]{:T(128)}, f32[512,2304]{1,0:T(8,128)}, s32[]{:T(128)}, bf16[4,512,512]{2,1,0:T(8,128)(2,1)}, bf16[4,1,512,2304]{3,2,1,0:T(8,128)(2,1)}, /*index=5*/s32[]{:T(128)}, s32[]{:T(128)}, s32[]{:T(128)}) while((s32[]{:T(128)}, f32[512,2304]{1,0:T(8,128)}, s32[]{:T(128)}, bf16[4,512,512]{2,1,0:T(8,128)(2,1)}, ...), condition=%wide.region_1.2_spmd, body=%wide.region_0.1_spmd.sunk | while | flops 1209139200 | bytes 12321911 | solution.py:29
  132.0 6.8 %convolution_add_fusion.2 = f32[512,2304]{1,0:T(8,128)} fusion(f32[512,2304]{1,0:T(8,128)} %get-tuple-element.90, bf16[4,1,512,2304]{3,2,1,0:T(8,128)(2,1)} %get-tuple-element.101, s32[]{:T(128)S(6)} %select_n.7, bf16[4,512,512]{2,1,0:T(8,128)(2,1)} %get-tuple-element.100), kind=kOutput, calls=%fused_computation.clone.1 | convolution fusion | flops 1209139200 | bytes 12321792 | tf_op jit(solution)/shard_map/while/body/dot_general | solution.py:26
  138.8 0.0 copy-start.1
  138.8 0.0 reduce-scatter.2.cloned.1.call-update
  138.8 0.7 copy-done.1
  139.5 116.1 %reduce-scatter.2.cloned.1.call-done = f32[1,64,2304]{2,1,0:T(8,128)} async-done(((f32[1,512,2304]{2,1,0:T(8,128)}), f32[1,64,2304]{2,1,0:T(8,128)}) %reduce-scatter.2.cloned.1.call-update) | async-done | bytes 589840 | tf_op jit(solution)/shard_map/reduce_scatter | solution.py:30
  255.6 1.8 add_convert_fusion
  (1 shorter events, 0.0 us)
Async XLA Ops:
  6.5 57.4 %copy-start = (bf16[1,2304,512]{2,1,0:T(8,128)(2,1)S(1)}, bf16[1,2304,512]{2,1,0:T(8,128)(2,1)}, u32[]{:S(2)}) copy-start(bf16[1,2304,512]{2,1,0:T(8,128)(2,1)} %param.8) | copy-start | bytes 7077892
  6.5 57.4 %all-gather.4.cloned.1.call-start = ((), (), s32[]{:S(2)}) async-start(), calls=%async_computation.2 | async-start | bytes 2654208 | tf_op jit(solution)/shard_map/all_gather | solution.py:10
  7.3 56.7 %copy-start.2 = (f32[1,512]{1,0:T(1,128)S(1)}, f32[1,512]{1,0:T(1,128)}, u32[]{:S(2)}) copy-start(f32[1,512]{1,0:T(1,128)} %param.9) | copy-start | bytes 6148
  7.3 122.2 %all-to-all-start = ((bf16[1,4,512,2304]{3,2,0,1:T(8,128)(2,1)}), bf16[1,4,512,2304]{3,2,0,1:T(8,128)(2,1)}, u32[]{:S(2)}, u32[]{:S(2)}) async-start(bf16[1,4,512,2304]{3,2,0,1:T(8,128)(2,1)} %bitcast.36), calls=%async_computation | async-start | bytes 18874368 | tf_op jit(solution)/shard_map/all_to_all | solution.py:20
  13.1 116.3 %all-gather.6.cloned.1.call-start = ((), (), s32[]{:S(2)}) async-start(), calls=%async_computation.4 | async-start | bytes 2621440 | tf_op jit(solution)/shard_map/all_gather | solution.py:21
  67.8 187.8 %reduce-scatter.2.cloned.1.call-start = ((), (), s32[]{:S(2)}) async-start(), calls=%async_computation.3 | async-start | bytes 5308416 | tf_op jit(solution)/shard_map/reduce_scatter | solution.py:30
  138.8 0.7 copy-start.1
Sparse Core Ops, SparseCore 0:
  9.5 54.3 all-gather.3
  67.9 32.4 all-gather.5
  138.9 116.5 reduce-scatter.1
where the time goes:
time: 264 us
  waiting for transfers between devices  229 us (87%)
  between operations  13.1 us (5%)
  matrix products  10.7 us (4%)
  starting transfers between devices  5.9 us (2%)
  local copies, waits for them, and re-layouts  3.21 us (1%)
    reduce_scatter x1, waiting for transfers between devices, per_device(): lax.psum_scatter(own_sum[None], 'feat', scatter_dimension=1, tiled=True)  116 us
    all_to_all x1, waiting for transfers between devices, per_device(): lax.all_to_all(dec_weight, 'layer', split_axis=1, concat_axis=0, tiled=True)  61.6 us
    all_gather x1, waiting for transfers between devices, per_device(): lax.all_gather(resid_in, 'feat', axis=1, tiled=True)[0]  50.8 us
    dot_general x1, matrix products, accumulate(): return running + jnp.dot(rows, weight, preferred_element_type=jnp.float32)  6.83 us
    all_to_all x1, starting transfers between devices, per_device(): lax.all_to_all(dec_weight, 'layer', split_axis=1, concat_axis=0, tiled=True)  5.82 us
  transfers between devices with their start and end apart: 4, of which 3 were waited for; matrix products, arithmetic and copies ran while one was open for 1% of the time, Pallas kernels for 0%

commit v1 on v0

--- a/solution.py
+++ b/solution.py
@@ -4,7 +4,7 @@
 from jax.sharding import PartitionSpec as P
 
 
-def per_device(resid_in, enc_weight, enc_bias, dec_weight, dec_bias):
+def gathered_form(resid_in, enc_weight, enc_bias, dec_weight, dec_bias):
     preact = (
         jnp.dot(
             lax.all_gather(resid_in, "feat", axis=1, tiled=True)[0],
@@ -31,7 +31,105 @@
     return (summed + dec_bias[:, None, :]).astype(jnp.bfloat16)
 
 
+def ring_of(size):
+    return list(range(0, size, 2)) + list(range(size - 1, 0, -2))
+
+
+def ring_form(size, resid_in, enc_weight, enc_bias, dec_weight, dec_bias):
+    far = size // 2
+    order = ring_of(size)
+    ahead = [(order[i], order[(i + 1) % size]) for i in range(size)]
+    back = [(b, a) for a, b in ahead]
+    swap = [(0, 1), (1, 0), (2, 3), (3, 2)]
+    over = [(0, 2), (1, 3)]
+
+    layer = lax.axis_index("layer")
+    core = layer % 2
+    rows = resid_in[0]
+    count = rows.shape[0]
+    half = count // 2
+
+    def decoder(weights, target):
+        return lax.dynamic_index_in_dim(weights[0], target, 0, keepdims=False)
+
+    give = jnp.stack([jnp.where(core == 0, decoder(dec_weight, jnp.minimum(layer + 1, 3)), 0), decoder(dec_weight, 3 - core)])
+    give = lax.optimization_barrier(give)
+    take = lax.ppermute(give, "layer", swap)
+    near = jnp.concatenate([decoder(dec_weight, layer), take[0]], axis=0)
+    upper = jnp.concatenate([decoder(dec_weight, 2 + core), take[1]], axis=0)
+    near, upper = lax.optimization_barrier((near, upper))
+
+    fwd = [rows]
+    bwd = [rows]
+    for _ in range(1, far):
+        fwd.append(lax.ppermute(fwd[-1], "feat", ahead))
+        bwd.append(lax.ppermute(bwd[-1], "feat", back))
+    ends = [lax.ppermute(fwd[-1][:half], "feat", ahead), lax.ppermute(bwd[-1][half:], "feat", back)]
+    chunks = [rows] + [jnp.concatenate([bwd[d], fwd[d]], axis=0) for d in range(1, far)] + [jnp.concatenate(ends, axis=0)]
+
+    made = []
+    for chunk in chunks:
+        preact = jnp.dot(chunk, enc_weight[0], preferred_element_type=jnp.float32) + enc_bias[0][None, :]
+        own = jnp.maximum(preact, 0.0).astype(jnp.bfloat16)
+        other = lax.ppermute(own, "layer", swap)
+        both = jnp.concatenate([own, other], axis=1)
+        pair = []
+        for w in (near, upper):
+            pair.append(jnp.dot(both, w, preferred_element_type=jnp.float32).astype(jnp.bfloat16))
+        made.append([lax.optimization_barrier(v) for v in pair])
+
+    def piece(which, distance, forward, part):
+        full = made[distance][which]
+        if distance == far:
+            return lax.optimization_barrier(full[part * half : (part + 1) * half])
+        first = (0 if forward else count) + part * half
+        return lax.optimization_barrier(full[first : first + half])
+
+    def plus(*values):
+        total = values[0].astype(jnp.float32)
+        for v in values[1:]:
+            total = total + v.astype(jnp.float32)
+        return total.astype(jnp.bfloat16)
+
+    ways = [(True, 0), (True, 1), (False, 0), (False, 1)]
+    begins = {w: far if w[0] == (w[1] == 0) else far - 1 for w in ways}
+
+    got = lax.ppermute(jnp.concatenate([made[1][1], made[0][1]], axis=0), "layer", over)
+    straight = got[2 * count :]
+    made[1][0] = lax.optimization_barrier(plus(made[1][0], got[: 2 * count]))
+
+    crossed = {}
+
+    def chain(which, way, stop):
+        forward, part = way
+        value = piece(which, begins[way], forward, part)
+        for distance in range(begins[way] - 1, stop - 1, -1):
+            got = lax.ppermute(value, "feat", ahead if forward else back)
+            if distance == 0:
+                return got
+            extra = [crossed[way]] if which == 0 and distance == CROSS else []
+            value = plus(got, piece(which, distance, forward, part), *extra)
+        return value
+
+    for pair in (((True, 1), (False, 0)), ((True, 0), (False, 1))):
+        got = lax.ppermute(jnp.concatenate([chain(1, w, CROSS) for w in pair], axis=0), "layer", over)
+        for i, w in enumerate(pair):
+            crossed[w] = lax.optimization_barrier(got[i * half : (i + 1) * half])
+    joined = [jnp.concatenate([chain(0, (f, part), 0) for part in (0, 1)], axis=0) for f in (True, False)]
+    total = sum(v.astype(jnp.float32) for v in joined + [straight, made[0][0]])
+    return (total + dec_bias)[None].astype(jnp.bfloat16)
+
+
+CROSS = 2
+
+
 def solution(mesh):
+    size, layers = mesh.shape["feat"], mesh.shape["layer"]
+    if layers == 4 and size % 2 == 0 and 6 <= size <= 16:
+        def per_device(*arrays):
+            return ring_form(size, *arrays)
+    else:
+        per_device = gathered_form
     return jax.shard_map(
         per_device,
         mesh=mesh,

time: 264 us -> 112 us (0.42)
  waiting for transfers between devices: 229 us -> 44.5 us
  starting transfers between devices: 5.9 us -> 39.7 us
  between operations: 13.1 us -> 0.49 us
  other arithmetic: 1.84 us -> 11.8 us
    reduce_scatter x1 -> x0, waiting for transfers between devices: 116 us -> none  [per_device(): lax.psum_scatter(own_sum[None], 'feat', scatter_dimension=1, tiled=True)]
    all_to_all x1 -> x0, waiting for transfers between devices: 61.6 us -> none  [per_device(): lax.all_to_all(dec_weight, 'layer', split_axis=1, concat_axis=0, tiled=True)]
    all_gather x2 -> x0, waiting for transfers between devices: 50.8 us -> none  [the longest x1 50.8 us: per_device(): lax.all_gather(resid_in, 'feat', axis=1, tiled=True)[0]]
    ppermute x0 -> x37, waiting for transfers between devices: none -> 44.5 us  [the longest x20 18.2 us: chain(): got = lax.ppermute(value, 'feat', ahead if forward else back)]
    ppermute x0 -> x37, starting transfers between devices: none -> 39.7 us  [the longest x20 22 us: chain(): got = lax.ppermute(value, 'feat', ahead if forward else back)]
    squeeze x0 -> x1, other arithmetic: none -> 6.76 us  [decoder(): return lax.dynamic_index_in_dim(weights[0], target, 0, keepdims=False)]
    all_to_all x1 -> x0, starting transfers between devices: 5.82 us -> none  [per_device(): lax.all_to_all(dec_weight, 'layer', split_axis=1, concat_axis=0, tiled=True)]
    squeeze x0 -> x1, local copies, waits for them, and re-layouts: none -> 2.97 us  [ring_form(): upper = jnp.concatenate([decoder(dec_weight, 2 + core), take[1]], axis=0)]
  transfers between devices with their start and end apart: 4 -> 37, of which waited for: 3 -> 15; matrix products, arithmetic and copies ran while one was open for 1% -> 15% of each run, Pallas kernels for 0% -> 0%
where the time goes in v1:
time: 112 us
  waiting for transfers between devices  44.5 us (40%)
  starting transfers between devices  39.7 us (35%)
  matrix products  11.9 us (11%)
  other arithmetic  11.8 us (11%)
  local copies, waits for them, and re-layouts  3.52 us (3%)
    ppermute x20, starting transfers between devices, chain(): got = lax.ppermute(value, 'feat', ahead if forward else back)  22 us
    ppermute x20, waiting for transfers between devices, chain(): got = lax.ppermute(value, 'feat', ahead if forward else back)  18.2 us
    ppermute x3, waiting for transfers between devices, ring_form(): fwd.append(lax.ppermute(fwd[-1], 'feat', ahead))  17.9 us
    dot_general x10, matrix products, ring_form(): jnp.dot(both, w, preferred_element_type=jnp.float32).astype(jnp.bfloat16)  8.45 us
    squeeze x1, other arithmetic, decoder(): return lax.dynamic_index_in_dim(weights[0], target, 0, keepdims=False)  6.76 us
    ppermute x3, starting transfers between devices, ring_form(): fwd.append(lax.ppermute(fwd[-1], 'feat', ahead))  5.93 us
    ppermute x2, waiting for transfers between devices, ring_form(): lax.ppermute(jnp.concatenate([chain(1, w, CROSS) for w in pair], axis=0),...  4.57 us
    ppermute x2, starting transfers between devices, ring_form(): lax.ppermute(jnp.concatenate([chain(1, w, CROSS) for w in pair], axis=0),...  4.21 us
  transfers between devices with their start and end apart: 37, of which 15 were waited for; matrix products, arithmetic and copies ran while one was open for 15% of the time, Pallas kernels for 0%

profile of v1, /device:TPU:0, one launch (start us, length us, event | category | flops | bytes accessed | tf_op | source)
XLA Modules:
  0.0 111.9 jit_solution(8688250726818043620)
XLA Ops:
  0.0 6.8 %dynamic-slice_bitcast_fusion = (bf16[512,2304]{1,0:T(8,128)(2,1)}, bf16[1,512,2304]{2,1,0:T(8,128)(2,1)S(1)}, bf16[512,2304]{1,0:T(8,128)(2,1)}, bf16[1,512,2304]{2,1,0:T(8,128)(2,1)S(1)}) fusion(bf16[1,4,512,2304]{3,2,1,0:T(8,128)(2,1)} %param.8, s32[]{:T(128)S(6)} %select_n.45, s32[]{:T(128)S(6)} %select_n.41, pred[]{:T(512)S(6)} %eq.5, s32[]{:T(128)S(6)} %select_n.38, ...), kind=kLoop, calls=%fused_computation.25 | loop fusion | flops 1179648 | bytes 18874384 | tf_op jit(solution)/shard_map/jit(dynamic_index_in_dim)/squeeze | solution.py:53
  6.8 2.6 %pad_maximum_fusion = bf16[2,512,2304]{2,1,0:T(8,128)(2,1)} fusion(bf16[1,512,2304]{2,1,0:T(8,128)(2,1)S(1)} %get-tuple-element.12, bf16[1,512,2304]{2,1,0:T(8,128)(2,1)S(1)} %get-tuple-element.10), kind=kLoop, calls=%fused_computation | loop fusion | flops 2359296 | bytes 9437184 | tf_op jit(solution)/shard_map/stack | solution.py:55
  9.8 2.6 %collective-permute-start = (bf16[64,2304]{1,0:T(8,128)(2,1)S(1)}, bf16[64,2304]{1,0:T(8,128)(2,1)S(1)}, u32[]{:S(2)}, u32[]{:S(2)}) collective-permute-start(bf16[64,2304]{1,0:T(8,128)(2,1)S(1)} %bitcast.69), channel_id=1, source_target_pairs={{0,8},{8,16},{16,24},{24,28},{28,20},{20,12},{12,4},{4,0},{1,9},{9... | collective-permute-start | bytes 884744 | tf_op jit(solution)/shard_map/ppermute | solution.py:65
  12.5 7.6 %collective-permute-done = bf16[64,2304]{1,0:T(8,128)(2,1)S(1)} collective-permute-done((bf16[64,2304]{1,0:T(8,128)(2,1)S(1)}, bf16[64,2304]{1,0:T(8,128)(2,1)S(1)}, u32[]{:S(2)}, u32[]{:S(2)}) %collective-permute-start) | collective-permute-done | bytes 294944 | tf_op jit(solution)/shard_map/ppermute | solution.py:65
  20.0 1.8 %collective-permute-start.1 = (bf16[64,2304]{1,0:T(8,128)(2,1)S(1)}, bf16[64,2304]{1,0:T(8,128)(2,1)}, u32[]{:S(2)}, u32[]{:S(2)}) collective-permute-start(bf16[64,2304]{1,0:T(8,128)(2,1)S(1)} %collective-permute-done), channel_id=1, source_target_pairs={{0,8},{8,16},{16,24},{24,28},{28,20},{20,12},{12,4},{4,0},{1,9},{9... | collective-permute-start | bytes 884744 | tf_op jit(solution)/shard_map/ppermute | solution.py:65
  22.7 6.2 %collective-permute-done.1 = bf16[64,2304]{1,0:T(8,128)(2,1)} collective-permute-done((bf16[64,2304]{1,0:T(8,128)(2,1)S(1)}, bf16[64,2304]{1,0:T(8,128)(2,1)}, u32[]{:S(2)}, u32[]{:S(2)}) %collective-permute-start.1) | collective-permute-done | bytes 294944 | tf_op jit(solution)/shard_map/ppermute | solution.py:65
  28.9 1.5 %collective-permute-start.2 = (bf16[64,2304]{1,0:T(8,128)(2,1)}, bf16[64,2304]{1,0:T(8,128)(2,1)S(1)}, u32[]{:S(2)}, u32[]{:S(2)}) collective-permute-start(bf16[64,2304]{1,0:T(8,128)(2,1)} %collective-permute-done.1), channel_id=1, source_target_pairs={{0,8},{8,16},{16,24},{24,28},{28,20},{20,12},{12,4},{4,0},{1,9},{9... | collective-permute-start | bytes 884744 | tf_op jit(solution)/shard_map/ppermute | solution.py:65
  31.5 1.4 %fusion.31 = bf16[128,512]{1,0:T(8,128)(2,1)S(1)} fusion(bf16[1,2304,512]{2,1,0:T(8,128)(2,1)S(1)} %copy-done, bf16[64,2304]{1,0:T(8,128)(2,1)} %collective-permute-done.1, bf16[64,2304]{1,0:T(8,128)(2,1)S(1)} %collective-permute-done.5, f32[512]{0:T(512)S(1)} %bitcast.73), kind=kOutput, calls=%fused_computation.37 | convolution fusion | flops 303366144 | bytes 3082240 | tf_op jit(solution)/shard_map/dot_general | solution.py:72
  33.0 4.1 %collective-permute-done.2 = bf16[64,2304]{1,0:T(8,128)(2,1)S(1)} collective-permute-done((bf16[64,2304]{1,0:T(8,128)(2,1)}, bf16[64,2304]{1,0:T(8,128)(2,1)S(1)}, u32[]{:S(2)}, u32[]{:S(2)}) %collective-permute-start.2) | collective-permute-done | bytes 294944 | tf_op jit(solution)/shard_map/ppermute | solution.py:65
  39.7 2.6 %collective-permute-done.3 = bf16[32,2304]{1,0:T(8,128)(2,1)S(1)} collective-permute-done((bf16[32,2304]{1,0:T(8,128)(2,1)S(1)}, bf16[32,2304]{1,0:T(8,128)(2,1)S(1)}, u32[]{:S(2)}, u32[]{:S(2)}) %collective-permute-start.3) | collective-permute-done | bytes 147488 | tf_op jit(solution)/shard_map/ppermute | solution.py:67
  42.3 1.3 %collective-permute-done.7 = bf16[32,2304]{1,0:T(8,128)(2,1)S(1)} collective-permute-done((bf16[32,2304]{1,0:T(8,128)(2,1)S(1)}, bf16[32,2304]{1,0:T(8,128)(2,1)S(1)}, u32[]{:S(2)}, u32[]{:S(2)}) %collective-permute-start.7) | collective-permute-done | bytes 147488 | tf_op jit(solution)/shard_map/ppermute | solution.py:67
  44.7 3.0 %slice_bitcast_fusion = (bf16[512,2304]{1,0:T(8,128)(2,1)S(1)}, bf16[512,2304]{1,0:T(8,128)(2,1)S(1)}) fusion(bf16[2,512,2304]{2,1,0:T(8,128)(2,1)} %collective-permute-done.9), kind=kLoop, calls=%fused_computation.13 | loop fusion | bytes 9437184 | tf_op jit(solution)/shard_map/squeeze | solution.py:59
  49.4 1.6 %collective-permute-start.25 = (bf16[32,2304]{1,0:T(8,128)(2,1)S(1)}, bf16[32,2304]{1,0:T(8,128)(2,1)S(1)}, u32[]{:S(2)}, u32[]{:S(2)}) collective-permute-start(bf16[32,2304]{1,0:T(8,128)(2,1)S(1)} %get-tuple-element.29), channel_id=1, source_target_pairs={{0,8},{8,16},{16,24},{24,28},{28,20},{20,12},{12,4},{4,0},{1,9},{9... | collective-permute-start | bytes 442376 | tf_op jit(solution)/shard_map/ppermute | solution.py:107
  55.9 3.4 %collective-permute-start.22 = (bf16[192,2304]{1,0:T(8,128)(2,1)S(1)}, bf16[192,2304]{1,0:T(8,128)(2,1)S(1)}, u32[]{:S(2)}, u32[]{:S(2)}) collective-permute-start(bf16[192,2304]{1,0:T(8,128)(2,1)S(1)} %pad_maximum_fusion.3), channel_id=1, source_target_pairs={{0,2},{1,3},{4,6},{5,7},{8,10},{9,11},{12,14},{13,15},{16,18},{17,... | collective-permute-start | bytes 2654216 | tf_op jit(solution)/shard_map/ppermute | solution.py:97
  62.6 1.6 %collective-permute-start.30 = (bf16[32,2304]{1,0:T(8,128)(2,1)S(1)}, bf16[32,2304]{1,0:T(8,128)(2,1)S(1)}, u32[]{:S(2)}, u32[]{:S(2)}) collective-permute-start(bf16[32,2304]{1,0:T(8,128)(2,1)S(1)} %get-tuple-element.15), channel_id=1, source_target_pairs={{8,0},{16,8},{24,16},{28,24},{20,28},{12,20},{4,12},{0,4},{9,1},{1... | collective-permute-start | bytes 442376 | tf_op jit(solution)/shard_map/ppermute | solution.py:107
  64.8 1.6 %collective-permute-start.16 = (bf16[32,2304]{1,0:T(8,128)(2,1)S(1)}, bf16[32,2304]{1,0:T(8,128)(2,1)S(1)}, u32[]{:S(2)}, u32[]{:S(2)}) collective-permute-start(bf16[32,2304]{1,0:T(8,128)(2,1)S(1)} %get-tuple-element.42), channel_id=1, source_target_pairs={{8,0},{16,8},{24,16},{28,24},{20,28},{12,20},{4,12},{0,4},{9,1},{1... | collective-permute-start | bytes 442376 | tf_op jit(solution)/shard_map/ppermute | solution.py:107
  66.4 1.6 %collective-permute-done.33 = bf16[32,2304]{1,0:T(8,128)(2,1)S(1)} collective-permute-done((bf16[32,2304]{1,0:T(8,128)(2,1)S(1)}, bf16[32,2304]{1,0:T(8,128)(2,1)S(1)}, u32[]{:S(2)}, u32[]{:S(2)}) %collective-permute-start.33) | collective-permute-done | bytes 147488 | tf_op jit(solution)/shard_map/ppermute | solution.py:107
  67.9 1.6 %collective-permute-start.10 = (bf16[32,2304]{1,0:T(8,128)(2,1)S(1)}, bf16[32,2304]{1,0:T(8,128)(2,1)S(1)}, u32[]{:S(2)}, u32[]{:S(2)}) collective-permute-start(bf16[32,2304]{1,0:T(8,128)(2,1)S(1)} %get-tuple-element.38), channel_id=1, source_target_pairs={{0,8},{8,16},{16,24},{24,28},{28,20},{20,12},{12,4},{4,0},{1,9},{9... | collective-permute-start | bytes 442376 | tf_op jit(solution)/shard_map/ppermute | solution.py:107
  71.4 1.5 %collective-permute-done.16 = bf16[32,2304]{1,0:T(8,128)(2,1)S(1)} collective-permute-done((bf16[32,2304]{1,0:T(8,128)(2,1)S(1)}, bf16[32,2304]{1,0:T(8,128)(2,1)S(1)}, u32[]{:S(2)}, u32[]{:S(2)}) %collective-permute-start.16) | collective-permute-done | bytes 147488 | tf_op jit(solution)/shard_map/ppermute | solution.py:107
  73.0 1.5 %collective-permute-start.27 = (bf16[64,2304]{1,0:T(8,128)(2,1)S(1)}, bf16[64,2304]{1,0:T(8,128)(2,1)S(1)}, u32[]{:S(2)}, u32[]{:S(2)}) collective-permute-start(bf16[64,2304]{1,0:T(8,128)(2,1)S(1)} %pad_maximum_fusion.5), channel_id=1, source_target_pairs={{0,2},{1,3},{4,6},{5,7},{8,10},{9,11},{12,14},{13,15},{16,18},{17,... | collective-permute-start | bytes 884744 | tf_op jit(solution)/shard_map/ppermute | solution.py:115
  74.5 1.6 %collective-permute-start.15 = (bf16[32,2304]{1,0:T(8,128)(2,1)S(1)}, bf16[32,2304]{1,0:T(8,128)(2,1)S(1)}, u32[]{:S(2)}, u32[]{:S(2)}) collective-permute-start(bf16[32,2304]{1,0:T(8,128)(2,1)S(1)} %add_convert_fusion.16), channel_id=1, source_target_pairs={{0,8},{8,16},{16,24},{24,28},{28,20},{20,12},{12,4},{4,0},{1,9},{9... | collective-permute-start | bytes 442376 | tf_op jit(solution)/shard_map/ppermute | solution.py:107
  76.2 3.5 %collective-permute-done.15 = bf16[32,2304]{1,0:T(8,128)(2,1)S(1)} collective-permute-done((bf16[32,2304]{1,0:T(8,128)(2,1)S(1)}, bf16[32,2304]{1,0:T(8,128)(2,1)S(1)}, u32[]{:S(2)}, u32[]{:S(2)}) %collective-permute-start.15) | collective-permute-done | bytes 147488 | tf_op jit(solution)/shard_map/ppermute | solution.py:107
  80.9 4.9 %collective-permute-done.17 = bf16[32,2304]{1,0:T(8,128)(2,1)S(1)} collective-permute-done((bf16[32,2304]{1,0:T(8,128)(2,1)S(1)}, bf16[32,2304]{1,0:T(8,128)(2,1)S(1)}, u32[]{:S(2)}, u32[]{:S(2)}) %collective-permute-start.17) | collective-permute-done | bytes 147488 | tf_op jit(solution)/shard_map/ppermute | solution.py:107
  86.0 1.9 %collective-permute-start.12 = (bf16[32,2304]{1,0:T(8,128)(2,1)S(1)}, bf16[32,2304]{1,0:T(8,128)(2,1)S(1)}, u32[]{:S(2)}, u32[]{:S(2)}) collective-permute-start(bf16[32,2304]{1,0:T(8,128)(2,1)S(1)} %add_convert_fusion.17), channel_id=1, source_target_pairs={{0,8},{8,16},{16,24},{24,28},{28,20},{20,12},{12,4},{4,0},{1,9},{9... | collective-permute-start | bytes 442376 | tf_op jit(solution)/shard_map/ppermute | solution.py:107
  88.0 2.7 %collective-permute-start.18 = (bf16[64,2304]{1,0:T(8,128)(2,1)S(1)}, bf16[64,2304]{1,0:T(8,128)(2,1)S(1)}, u32[]{:S(2)}, u32[]{:S(2)}) collective-permute-start(bf16[64,2304]{1,0:T(8,128)(2,1)S(1)} %pad_maximum_fusion.4), channel_id=1, source_target_pairs={{0,2},{1,3},{4,6},{5,7},{8,10},{9,11},{12,14},{13,15},{16,18},{17,... | collective-permute-start | bytes 884744 | tf_op jit(solution)/shard_map/ppermute | solution.py:115
  91.3 4.6 %collective-permute-done.18 = bf16[64,2304]{1,0:T(8,128)(2,1)S(1)} collective-permute-done((bf16[64,2304]{1,0:T(8,128)(2,1)S(1)}, bf16[64,2304]{1,0:T(8,128)(2,1)S(1)}, u32[]{:S(2)}, u32[]{:S(2)}) %collective-permute-start.18) | collective-permute-done | bytes 294944 | tf_op jit(solution)/shard_map/ppermute | solution.py:115
  95.9 1.6 %collective-permute-start.28 = (bf16[32,2304]{1,0:T(8,128)(2,1)S(1)}, bf16[32,2304]{1,0:T(8,128)(2,1)S(1)}, u32[]{:S(2)}, u32[]{:S(2)}) collective-permute-start(bf16[32,2304]{1,0:T(8,128)(2,1)S(1)} %add_convert_fusion.8), channel_id=1, source_target_pairs={{0,8},{8,16},{16,24},{24,28},{28,20},{20,12},{12,4},{4,0},{1,9},{9... | collective-permute-start | bytes 442376 | tf_op jit(solution)/shard_map/ppermute | solution.py:107
  98.1 1.6 %collective-permute-start.19 = (bf16[32,2304]{1,0:T(8,128)(2,1)S(1)}, bf16[32,2304]{1,0:T(8,128)(2,1)S(1)}, u32[]{:S(2)}, u32[]{:S(2)}) collective-permute-start(bf16[32,2304]{1,0:T(8,128)(2,1)S(1)} %add_convert_fusion.12), channel_id=1, source_target_pairs={{0,8},{8,16},{16,24},{24,28},{28,20},{20,12},{12,4},{4,0},{1,9},{9... | collective-permute-start | bytes 442376 | tf_op jit(solution)/shard_map/ppermute | solution.py:107
  100.5 3.1 %collective-permute-done.35 = bf16[32,2304]{1,0:T(8,128)(2,1)S(1)} collective-permute-done((bf16[32,2304]{1,0:T(8,128)(2,1)S(1)}, bf16[32,2304]{1,0:T(8,128)(2,1)S(1)}, u32[]{:S(2)}, u32[]{:S(2)}) %collective-permute-start.35) | collective-permute-done | bytes 147488 | tf_op jit(solution)/shard_map/ppermute | solution.py:107
  104.2 1.6 %collective-permute-start.23 = (bf16[32,2304]{1,0:T(8,128)(2,1)S(1)}, bf16[32,2304]{1,0:T(8,128)(2,1)S(1)}, u32[]{:S(2)}, u32[]{:S(2)}) collective-permute-start(bf16[32,2304]{1,0:T(8,128)(2,1)S(1)} %add_convert_fusion.11), channel_id=1, source_target_pairs={{0,8},{8,16},{16,24},{24,28},{28,20},{20,12},{12,4},{4,0},{1,9},{9... | collective-permute-start | bytes 442376 | tf_op jit(solution)/shard_map/ppermute | solution.py:107
  105.8 1.9 %collective-permute-start.29 = (bf16[32,2304]{1,0:T(8,128)(2,1)S(1)}, bf16[32,2304]{1,0:T(8,128)(2,1)S(1)}, u32[]{:S(2)}, u32[]{:S(2)}) collective-permute-start(bf16[32,2304]{1,0:T(8,128)(2,1)S(1)} %add_convert_fusion.7), channel_id=1, source_target_pairs={{0,8},{8,16},{16,24},{24,28},{28,20},{20,12},{12,4},{4,0},{1,9},{9... | collective-permute-start | bytes 442376 | tf_op jit(solution)/shard_map/ppermute | solution.py:107
  109.4 1.7 %collective-permute-done.29 = bf16[32,2304]{1,0:T(8,128)(2,1)S(1)} collective-permute-done((bf16[32,2304]{1,0:T(8,128)(2,1)S(1)}, bf16[32,2304]{1,0:T(8,128)(2,1)S(1)}, u32[]{:S(2)}, u32[]{:S(2)}) %collective-permute-start.29) | collective-permute-done | bytes 147488 | tf_op jit(solution)/shard_map/ppermute | solution.py:107
  (106 shorter events, 24.9 us)
Async XLA Ops:
  9.3 34.8 %collective-permute-start.9 = (bf16[2,512,2304]{2,1,0:T(8,128)(2,1)}, bf16[2,512,2304]{2,1,0:T(8,128)(2,1)}, u32[]{:S(2)}, u32[]{:S(2)}) collective-permute-start(bf16[2,512,2304]{2,1,0:T(8,128)(2,1)} %pad_maximum_fusion), channel_id=1, source_target_pairs={{0,1},{1,0},{2,3},{3,2},{4,5},{5,4},{6,7},{7,6},{8,9},{9,8},{10,11... | collective-permute-start | bytes 14155784 | tf_op jit(solution)/shard_map/ppermute | solution.py:57
  9.8 10.2 %collective-permute-start = (bf16[64,2304]{1,0:T(8,128)(2,1)S(1)}, bf16[64,2304]{1,0:T(8,128)(2,1)S(1)}, u32[]{:S(2)}, u32[]{:S(2)}) collective-permute-start(bf16[64,2304]{1,0:T(8,128)(2,1)S(1)} %bitcast.69), channel_id=1, source_target_pairs={{0,8},{8,16},{16,24},{24,28},{28,20},{20,12},{12,4},{4,0},{1,9},{9... | collective-permute-start | bytes 884744 | tf_op jit(solution)/shard_map/ppermute | solution.py:65
  12.4 9.4 %collective-permute-start.4 = (bf16[64,2304]{1,0:T(8,128)(2,1)S(1)}, bf16[64,2304]{1,0:T(8,128)(2,1)S(1)}, u32[]{:S(2)}, u32[]{:S(2)}) collective-permute-start(bf16[64,2304]{1,0:T(8,128)(2,1)S(1)} %bitcast.70), channel_id=1, source_target_pairs={{8,0},{16,8},{24,16},{28,24},{20,28},{12,20},{4,12},{0,4},{9,1},{1... | collective-permute-start | bytes 884744 | tf_op jit(solution)/shard_map/ppermute | solution.py:66
  20.0 8.9 %collective-permute-start.1 = (bf16[64,2304]{1,0:T(8,128)(2,1)S(1)}, bf16[64,2304]{1,0:T(8,128)(2,1)}, u32[]{:S(2)}, u32[]{:S(2)}) collective-permute-start(bf16[64,2304]{1,0:T(8,128)(2,1)S(1)} %collective-permute-done), channel_id=1, source_target_pairs={{0,8},{8,16},{16,24},{24,28},{28,20},{20,12},{12,4},{4,0},{1,9},{9... | collective-permute-start | bytes 884744 | tf_op jit(solution)/shard_map/ppermute | solution.py:65
  21.8 8.6 %collective-permute-start.5 = (bf16[64,2304]{1,0:T(8,128)(2,1)S(1)}, bf16[64,2304]{1,0:T(8,128)(2,1)S(1)}, u32[]{:S(2)}, u32[]{:S(2)}) collective-permute-start(bf16[64,2304]{1,0:T(8,128)(2,1)S(1)} %collective-permute-done.4), channel_id=1, source_target_pairs={{8,0},{16,8},{24,16},{28,24},{20,28},{12,20},{4,12},{0,4},{9,1},{1... | collective-permute-start | bytes 884744 | tf_op jit(solution)/shard_map/ppermute | solution.py:66
  22.6 32.3 %collective-permute-start.21 = (bf16[64,512]{1,0:T(8,128)(2,1)S(1)}, bf16[64,512]{1,0:T(8,128)(2,1)S(1)}, u32[]{:S(2)}, u32[]{:S(2)}) collective-permute-start(bf16[64,512]{1,0:T(8,128)(2,1)S(1)} %fusion.49), channel_id=1, source_target_pairs={{0,1},{1,0},{2,3},{3,2},{4,5},{5,4},{6,7},{7,6},{8,9},{9,8},{10,11... | collective-permute-start | bytes 196616 | tf_op jit(solution)/shard_map/ppermute | solution.py:74
  28.9 8.1 %collective-permute-start.2 = (bf16[64,2304]{1,0:T(8,128)(2,1)}, bf16[64,2304]{1,0:T(8,128)(2,1)S(1)}, u32[]{:S(2)}, u32[]{:S(2)}) collective-permute-start(bf16[64,2304]{1,0:T(8,128)(2,1)} %collective-permute-done.1), channel_id=1, source_target_pairs={{0,8},{8,16},{16,24},{24,28},{28,20},{20,12},{12,4},{4,0},{1,9},{9... | collective-permute-start | bytes 884744 | tf_op jit(solution)/shard_map/ppermute | solution.py:65
  30.4 7.9 %collective-permute-start.6 = (bf16[64,2304]{1,0:T(8,128)(2,1)S(1)}, bf16[64,2304]{1,0:T(8,128)(2,1)S(1)}, u32[]{:S(2)}, u32[]{:S(2)}) collective-permute-start(bf16[64,2304]{1,0:T(8,128)(2,1)S(1)} %collective-permute-done.5), channel_id=1, source_target_pairs={{8,0},{16,8},{24,16},{28,24},{20,28},{12,20},{4,12},{0,4},{9,1},{1... | collective-permute-start | bytes 884744 | tf_op jit(solution)/shard_map/ppermute | solution.py:66
  31.4 22.7 %collective-permute-start.20 = (bf16[128,512]{1,0:T(8,128)(2,1)S(1)}, bf16[128,512]{1,0:T(8,128)(2,1)S(1)}, u32[]{:S(2)}, u32[]{:S(2)}) collective-permute-start(bf16[128,512]{1,0:T(8,128)(2,1)S(1)} %fusion.34), channel_id=1, source_target_pairs={{0,1},{1,0},{2,3},{3,2},{4,5},{5,4},{6,7},{7,6},{8,9},{9,8},{10,11... | collective-permute-start | bytes 393224 | tf_op jit(solution)/shard_map/ppermute | solution.py:74
  37.1 5.2 %collective-permute-start.3 = (bf16[32,2304]{1,0:T(8,128)(2,1)S(1)}, bf16[32,2304]{1,0:T(8,128)(2,1)S(1)}, u32[]{:S(2)}, u32[]{:S(2)}) collective-permute-start(bf16[32,2304]{1,0:T(8,128)(2,1)S(1)} %slice.136), channel_id=1, source_target_pairs={{0,8},{8,16},{16,24},{24,28},{28,20},{20,12},{12,4},{4,0},{1,9},{9... | collective-permute-start | bytes 442376 | tf_op jit(solution)/shard_map/ppermute | solution.py:67
  38.4 5.2 %collective-permute-start.7 = (bf16[32,2304]{1,0:T(8,128)(2,1)S(1)}, bf16[32,2304]{1,0:T(8,128)(2,1)S(1)}, u32[]{:S(2)}, u32[]{:S(2)}) collective-permute-start(bf16[32,2304]{1,0:T(8,128)(2,1)S(1)} %slice.137), channel_id=1, source_target_pairs={{8,0},{16,8},{24,16},{28,24},{20,28},{12,20},{4,12},{0,4},{9,1},{1... | collective-permute-start | bytes 442376 | tf_op jit(solution)/shard_map/ppermute | solution.py:67
  42.3 8.8 %collective-permute-start.13 = (bf16[128,512]{1,0:T(8,128)(2,1)S(1)}, bf16[128,512]{1,0:T(8,128)(2,1)S(1)}, u32[]{:S(2)}, u32[]{:S(2)}) collective-permute-start(bf16[128,512]{1,0:T(8,128)(2,1)S(1)} %fusion.31), channel_id=1, source_target_pairs={{0,1},{1,0},{2,3},{3,2},{4,5},{5,4},{6,7},{7,6},{8,9},{9,8},{10,11... | collective-permute-start | bytes 393224 | tf_op jit(solution)/shard_map/ppermute | solution.py:74
  44.2 16.0 %collective-permute-start.8 = (bf16[64,512]{1,0:T(8,128)(2,1)S(1)}, bf16[64,512]{1,0:T(8,128)(2,1)S(1)}, u32[]{:S(2)}, u32[]{:S(2)}) collective-permute-start(bf16[64,512]{1,0:T(8,128)(2,1)S(1)} %fusion.52), channel_id=1, source_target_pairs={{0,1},{1,0},{2,3},{3,2},{4,5},{5,4},{6,7},{7,6},{8,9},{9,8},{10,11... | collective-permute-start | bytes 196616 | tf_op jit(solution)/shard_map/ppermute | solution.py:74
  49.4 14.8 %collective-permute-start.25 = (bf16[32,2304]{1,0:T(8,128)(2,1)S(1)}, bf16[32,2304]{1,0:T(8,128)(2,1)S(1)}, u32[]{:S(2)}, u32[]{:S(2)}) collective-permute-start(bf16[32,2304]{1,0:T(8,128)(2,1)S(1)} %get-tuple-element.29), channel_id=1, source_target_pairs={{0,8},{8,16},{16,24},{24,28},{28,20},{20,12},{12,4},{4,0},{1,9},{9... | collective-permute-start | bytes 442376 | tf_op jit(solution)/shard_map/ppermute | solution.py:107
  51.9 12.9 %collective-permute-start.26 = (bf16[32,2304]{1,0:T(8,128)(2,1)S(1)}, bf16[32,2304]{1,0:T(8,128)(2,1)S(1)}, u32[]{:S(2)}, u32[]{:S(2)}) collective-permute-start(bf16[32,2304]{1,0:T(8,128)(2,1)S(1)} %get-tuple-element.28), channel_id=1, source_target_pairs={{8,0},{16,8},{24,16},{28,24},{20,28},{12,20},{4,12},{0,4},{9,1},{1... | collective-permute-start | bytes 442376 | tf_op jit(solution)/shard_map/ppermute | solution.py:107
  55.9 43.8 %collective-permute-start.22 = (bf16[192,2304]{1,0:T(8,128)(2,1)S(1)}, bf16[192,2304]{1,0:T(8,128)(2,1)S(1)}, u32[]{:S(2)}, u32[]{:S(2)}) collective-permute-start(bf16[192,2304]{1,0:T(8,128)(2,1)S(1)} %pad_maximum_fusion.3), channel_id=1, source_target_pairs={{0,2},{1,3},{4,6},{5,7},{8,10},{9,11},{12,14},{13,15},{16,18},{17,... | collective-permute-start | bytes 2654216 | tf_op jit(solution)/shard_map/ppermute | solution.py:97
  61.2 6.8 %collective-permute-start.33 = (bf16[32,2304]{1,0:T(8,128)(2,1)S(1)}, bf16[32,2304]{1,0:T(8,128)(2,1)S(1)}, u32[]{:S(2)}, u32[]{:S(2)}) collective-permute-start(bf16[32,2304]{1,0:T(8,128)(2,1)S(1)} %get-tuple-element.37), channel_id=1, source_target_pairs={{8,0},{16,8},{24,16},{28,24},{20,28},{12,20},{4,12},{0,4},{9,1},{1... | collective-permute-start | bytes 442376 | tf_op jit(solution)/shard_map/ppermute | solution.py:107
  62.6 25.3 %collective-permute-start.30 = (bf16[32,2304]{1,0:T(8,128)(2,1)S(1)}, bf16[32,2304]{1,0:T(8,128)(2,1)S(1)}, u32[]{:S(2)}, u32[]{:S(2)}) collective-permute-start(bf16[32,2304]{1,0:T(8,128)(2,1)S(1)} %get-tuple-element.15), channel_id=1, source_target_pairs={{8,0},{16,8},{24,16},{28,24},{20,28},{12,20},{4,12},{0,4},{9,1},{1... | collective-permute-start | bytes 442376 | tf_op jit(solution)/shard_map/ppermute | solution.py:107
  64.2 6.5 %collective-permute-start.14 = (bf16[32,2304]{1,0:T(8,128)(2,1)S(1)}, bf16[32,2304]{1,0:T(8,128)(2,1)S(1)}, u32[]{:S(2)}, u32[]{:S(2)}) collective-permute-start(bf16[32,2304]{1,0:T(8,128)(2,1)S(1)} %get-tuple-element.41), channel_id=1, source_target_pairs={{0,8},{8,16},{16,24},{24,28},{28,20},{20,12},{12,4},{4,0},{1,9},{9... | collective-permute-start | bytes 442376 | tf_op jit(solution)/shard_map/ppermute | solution.py:107
  64.8 8.2 %collective-permute-start.16 = (bf16[32,2304]{1,0:T(8,128)(2,1)S(1)}, bf16[32,2304]{1,0:T(8,128)(2,1)S(1)}, u32[]{:S(2)}, u32[]{:S(2)}) collective-permute-start(bf16[32,2304]{1,0:T(8,128)(2,1)S(1)} %get-tuple-element.42), channel_id=1, source_target_pairs={{8,0},{16,8},{24,16},{28,24},{20,28},{12,20},{4,12},{0,4},{9,1},{1... | collective-permute-start | bytes 442376 | tf_op jit(solution)/shard_map/ppermute | solution.py:107
  67.9 6.6 %collective-permute-start.10 = (bf16[32,2304]{1,0:T(8,128)(2,1)S(1)}, bf16[32,2304]{1,0:T(8,128)(2,1)S(1)}, u32[]{:S(2)}, u32[]{:S(2)}) collective-permute-start(bf16[32,2304]{1,0:T(8,128)(2,1)S(1)} %get-tuple-element.38), channel_id=1, source_target_pairs={{0,8},{8,16},{16,24},{24,28},{28,20},{20,12},{12,4},{4,0},{1,9},{9... | collective-permute-start | bytes 442376 | tf_op jit(solution)/shard_map/ppermute | solution.py:107
  70.7 20.1 %collective-permute-start.24 = (bf16[32,2304]{1,0:T(8,128)(2,1)S(1)}, bf16[32,2304]{1,0:T(8,128)(2,1)S(1)}, u32[]{:S(2)}, u32[]{:S(2)}) collective-permute-start(bf16[32,2304]{1,0:T(8,128)(2,1)S(1)} %get-tuple-element.17), channel_id=1, source_target_pairs={{0,8},{8,16},{16,24},{24,28},{28,20},{20,12},{12,4},{4,0},{1,9},{9... | collective-permute-start | bytes 442376 | tf_op jit(solution)/shard_map/ppermute | solution.py:107
  73.0 13.1 %collective-permute-start.27 = (bf16[64,2304]{1,0:T(8,128)(2,1)S(1)}, bf16[64,2304]{1,0:T(8,128)(2,1)S(1)}, u32[]{:S(2)}, u32[]{:S(2)}) collective-permute-start(bf16[64,2304]{1,0:T(8,128)(2,1)S(1)} %pad_maximum_fusion.5), channel_id=1, source_target_pairs={{0,2},{1,3},{4,6},{5,7},{8,10},{9,11},{12,14},{13,15},{16,18},{17,... | collective-permute-start | bytes 884744 | tf_op jit(solution)/shard_map/ppermute | solution.py:115
  79.7 6.0 %collective-permute-start.17 = (bf16[32,2304]{1,0:T(8,128)(2,1)S(1)}, bf16[32,2304]{1,0:T(8,128)(2,1)S(1)}, u32[]{:S(2)}, u32[]{:S(2)}) collective-permute-start(bf16[32,2304]{1,0:T(8,128)(2,1)S(1)} %add_convert_fusion.14), channel_id=1, source_target_pairs={{8,0},{16,8},{24,16},{28,24},{20,28},{12,20},{4,12},{0,4},{9,1},{1... | collective-permute-start | bytes 442376 | tf_op jit(solution)/shard_map/ppermute | solution.py:107
  85.8 11.7 %collective-permute-start.34 = (bf16[32,2304]{1,0:T(8,128)(2,1)S(1)}, bf16[32,2304]{1,0:T(8,128)(2,1)S(1)}, u32[]{:S(2)}, u32[]{:S(2)}) collective-permute-start(bf16[32,2304]{1,0:T(8,128)(2,1)S(1)} %add_convert_fusion.4), channel_id=1, source_target_pairs={{8,0},{16,8},{24,16},{28,24},{20,28},{12,20},{4,12},{0,4},{9,1},{1... | collective-permute-start | bytes 442376 | tf_op jit(solution)/shard_map/ppermute | solution.py:107
  86.0 12.0 %collective-permute-start.12 = (bf16[32,2304]{1,0:T(8,128)(2,1)S(1)}, bf16[32,2304]{1,0:T(8,128)(2,1)S(1)}, u32[]{:S(2)}, u32[]{:S(2)}) collective-permute-start(bf16[32,2304]{1,0:T(8,128)(2,1)S(1)} %add_convert_fusion.17), channel_id=1, source_target_pairs={{0,8},{8,16},{16,24},{24,28},{28,20},{20,12},{12,4},{4,0},{1,9},{9... | collective-permute-start | bytes 442376 | tf_op jit(solution)/shard_map/ppermute | solution.py:107
  88.0 7.9 %collective-permute-start.18 = (bf16[64,2304]{1,0:T(8,128)(2,1)S(1)}, bf16[64,2304]{1,0:T(8,128)(2,1)S(1)}, u32[]{:S(2)}, u32[]{:S(2)}) collective-permute-start(bf16[64,2304]{1,0:T(8,128)(2,1)S(1)} %pad_maximum_fusion.4), channel_id=1, source_target_pairs={{0,2},{1,3},{4,6},{5,7},{8,10},{9,11},{12,14},{13,15},{16,18},{17,... | collective-permute-start | bytes 884744 | tf_op jit(solution)/shard_map/ppermute | solution.py:115
  90.7 9.2 %collective-permute-start.31 = (bf16[32,2304]{1,0:T(8,128)(2,1)S(1)}, bf16[32,2304]{1,0:T(8,128)(2,1)S(1)}, u32[]{:S(2)}, u32[]{:S(2)}) collective-permute-start(bf16[32,2304]{1,0:T(8,128)(2,1)S(1)} %add_convert_fusion.6), channel_id=1, source_target_pairs={{8,0},{16,8},{24,16},{28,24},{20,28},{12,20},{4,12},{0,4},{9,1},{1... | collective-permute-start | bytes 442376 | tf_op jit(solution)/shard_map/ppermute | solution.py:107
  95.9 9.9 %collective-permute-start.28 = (bf16[32,2304]{1,0:T(8,128)(2,1)S(1)}, bf16[32,2304]{1,0:T(8,128)(2,1)S(1)}, u32[]{:S(2)}, u32[]{:S(2)}) collective-permute-start(bf16[32,2304]{1,0:T(8,128)(2,1)S(1)} %add_convert_fusion.8), channel_id=1, source_target_pairs={{0,8},{8,16},{16,24},{24,28},{28,20},{20,12},{12,4},{4,0},{1,9},{9... | collective-permute-start | bytes 442376 | tf_op jit(solution)/shard_map/ppermute | solution.py:107
  97.6 6.0 %collective-permute-start.35 = (bf16[32,2304]{1,0:T(8,128)(2,1)S(1)}, bf16[32,2304]{1,0:T(8,128)(2,1)S(1)}, u32[]{:S(2)}, u32[]{:S(2)}) collective-permute-start(bf16[32,2304]{1,0:T(8,128)(2,1)S(1)} %add_convert_fusion.3), channel_id=1, source_target_pairs={{8,0},{16,8},{24,16},{28,24},{20,28},{12,20},{4,12},{0,4},{9,1},{1... | collective-permute-start | bytes 442376 | tf_op jit(solution)/shard_map/ppermute | solution.py:107
  98.1 6.0 %collective-permute-start.19 = (bf16[32,2304]{1,0:T(8,128)(2,1)S(1)}, bf16[32,2304]{1,0:T(8,128)(2,1)S(1)}, u32[]{:S(2)}, u32[]{:S(2)}) collective-permute-start(bf16[32,2304]{1,0:T(8,128)(2,1)S(1)} %add_convert_fusion.12), channel_id=1, source_target_pairs={{0,8},{8,16},{16,24},{24,28},{28,20},{20,12},{12,4},{4,0},{1,9},{9... | collective-permute-start | bytes 442376 | tf_op jit(solution)/shard_map/ppermute | solution.py:107
  100.0 8.7 %collective-permute-start.32 = (bf16[32,2304]{1,0:T(8,128)(2,1)S(1)}, bf16[32,2304]{1,0:T(8,128)(2,1)S(1)}, u32[]{:S(2)}, u32[]{:S(2)}) collective-permute-start(bf16[32,2304]{1,0:T(8,128)(2,1)S(1)} %add_convert_fusion.5), channel_id=1, source_target_pairs={{8,0},{16,8},{24,16},{28,24},{20,28},{12,20},{4,12},{0,4},{9,1},{1... | collective-permute-start | bytes 442376 | tf_op jit(solution)/shard_map/ppermute | solution.py:107
  (11 other events, 86.9 us)

commit v2 on v1

--- a/solution.py
+++ b/solution.py
@@ -1,6 +1,8 @@
 import jax
 import jax.numpy as jnp
 from jax import lax
+from jax.experimental import pallas as pl
+from jax.experimental.pallas import tpu as pltpu
 from jax.sharding import PartitionSpec as P
 
 
@@ -31,6 +33,17 @@
     return (summed + dec_bias[:, None, :]).astype(jnp.bfloat16)
 
 
+def spread(bias, count):
+    def body(bias_ref, out_ref):
+        out_ref[...] = jnp.broadcast_to(bias_ref[...], out_ref.shape)
+
+    return pl.pallas_call(
+        body,
+        out_shape=jax.ShapeDtypeStruct((count, bias.shape[1]), bias.dtype),
+        compiler_params=pltpu.CompilerParams(vmem_limit_bytes=2**21),
+    )(bias)
+
+
 def ring_of(size):
     return list(range(0, size, 2)) + list(range(size - 1, 0, -2))
 
@@ -48,6 +61,8 @@
     rows = resid_in[0]
     count = rows.shape[0]
     half = count // 2
+
+    bias_rows = spread(dec_bias, count)
 
     def decoder(weights, target):
         return lax.dynamic_index_in_dim(weights[0], target, 0, keepdims=False)
@@ -117,7 +132,7 @@
             crossed[w] = lax.optimization_barrier(got[i * half : (i + 1) * half])
     joined = [jnp.concatenate([chain(0, (f, part), 0) for part in (0, 1)], axis=0) for f in (True, False)]
     total = sum(v.astype(jnp.float32) for v in joined + [straight, made[0][0]])
-    return (total + dec_bias)[None].astype(jnp.bfloat16)
+    return (total + bias_rows)[None].astype(jnp.bfloat16)
 
 
 CROSS = 2

time: 112 us -> 104 us (0.929)
  other arithmetic: 11.8 us -> 7.45 us
  local copies, waits for them, and re-layouts: 3.52 us -> 0.64 us
    squeeze x1, local copies, waits for them, and re-layouts: 2.97 us -> 0.3 us  [ring_form(): upper = jnp.concatenate([decoder(dec_weight, 2 + core), take[1]], axis=0)]
    squeeze x1, other arithmetic: 6.76 us -> 4.52 us  [decoder(): return lax.dynamic_index_in_dim(weights[0], target, 0, keepdims=False)]
    another operation x1, other arithmetic: 2.57 us -> 0.43 us  [ring_form(): jnp.stack([jnp.where(core == 0, decoder(dec_weight, jnp.minimum(layer + 1...]
  transfers between devices with their start and end apart: 37 -> 37, of which waited for: 15 -> 16; matrix products, arithmetic and copies ran while one was open for 15% -> 13% of each run, Pallas kernels for 0% -> 0%
where the time goes in v2:
time: 104 us; the launch traced here: 103 us
  waiting for transfers between devices  43.4 us (42%)
  starting transfers between devices  40.5 us (39%)
  matrix products  10.9 us (10%)
  other arithmetic  7.45 us (7%)
    ppermute x20, starting transfers between devices, chain(): got = lax.ppermute(value, 'feat', ahead if forward else back)  22.5 us
    ppermute x20, waiting for transfers between devices, chain(): got = lax.ppermute(value, 'feat', ahead if forward else back)  18 us
    ppermute x3, waiting for transfers between devices, ring_form(): fwd.append(lax.ppermute(fwd[-1], 'feat', ahead))  17.4 us
    dot_general x10, matrix products, ring_form(): jnp.dot(both, w, preferred_element_type=jnp.float32).astype(jnp.bfloat16)  8.44 us
    ppermute x3, starting transfers between devices, ring_form(): fwd.append(lax.ppermute(fwd[-1], 'feat', ahead))  6.3 us
    squeeze x1, other arithmetic, decoder(): return lax.dynamic_index_in_dim(weights[0], target, 0, keepdims=False)  4.52 us
    ppermute x2, starting transfers between devices, ring_form(): lax.ppermute(jnp.concatenate([chain(1, w, CROSS) for w in pair], axis=0),...  4.18 us
    ppermute x2, waiting for transfers between devices, ring_form(): lax.ppermute(jnp.concatenate([chain(1, w, CROSS) for w in pair], axis=0),...  4.07 us
  transfers between devices with their start and end apart: 37, of which 16 were waited for; matrix products, arithmetic and copies ran while one was open for 13% of the time, Pallas kernels for 0%

profile of v2, /device:TPU:0, one launch (start us, length us, event | category | flops | bytes accessed | tf_op | source)
XLA Modules:
  0.0 103.5 jit_solution(3754032898324209435)
XLA Ops:
  0.0 4.5 %dynamic-slice_bitcast_fusion = (bf16[512,2304]{1,0:T(8,128)(2,1)S(1)}, bf16[1,512,2304]{2,1,0:T(8,128)(2,1)S(1)}, bf16[512,2304]{1,0:T(8,128)(2,1)S(1)}, bf16[1,512,2304]{2,1,0:T(8,128)(2,1)S(1)}) fusion(bf16[1,4,512,2304]{3,2,1,0:T(8,128)(2,1)} %param.8, s32[]{:T(128)S(6)} %select_n.45, s32[]{:T(128)S(6)} %select_n.41, pred[]{:T(512)S(6)} %eq.5, ...), kind=kLoop, calls=%fused_computation.25 | loop fusion | flops 1179648 | bytes 18874384 | tf_op jit(solution)/shard_map/jit(dynamic_index_in_dim)/squeeze | solution.py:68
  5.6 3.0 %collective-permute-start = (bf16[64,2304]{1,0:T(8,128)(2,1)S(1)}, bf16[64,2304]{1,0:T(8,128)(2,1)S(1)}, u32[]{:S(2)}, u32[]{:S(2)}) collective-permute-start(bf16[64,2304]{1,0:T(8,128)(2,1)S(1)} %bitcast.69), channel_id=1, source_target_pairs={{0,8},{8,16},{16,24},{24,28},{28,20},{20,12},{12,4},{4,0},{1,9},{9... | collective-permute-start | bytes 884744 | tf_op jit(solution)/shard_map/ppermute | solution.py:80
  8.5 7.2 %collective-permute-done = bf16[64,2304]{1,0:T(8,128)(2,1)S(1)} collective-permute-done((bf16[64,2304]{1,0:T(8,128)(2,1)S(1)}, bf16[64,2304]{1,0:T(8,128)(2,1)S(1)}, u32[]{:S(2)}, u32[]{:S(2)}) %collective-permute-start) | collective-permute-done | bytes 294944 | tf_op jit(solution)/shard_map/ppermute | solution.py:80
  15.7 1.8 %collective-permute-start.1 = (bf16[64,2304]{1,0:T(8,128)(2,1)S(1)}, bf16[64,2304]{1,0:T(8,128)(2,1)S(1)}, u32[]{:S(2)}, u32[]{:S(2)}) collective-permute-start(bf16[64,2304]{1,0:T(8,128)(2,1)S(1)} %collective-permute-done), channel_id=1, source_target_pairs={{0,8},{8,16},{16,24},{24,28},{28,20},{20,12},{12,4},{4,0},{1,9},{9... | collective-permute-start | bytes 884744 | tf_op jit(solution)/shard_map/ppermute | solution.py:80
  18.4 5.7 %collective-permute-done.1 = bf16[64,2304]{1,0:T(8,128)(2,1)S(1)} collective-permute-done((bf16[64,2304]{1,0:T(8,128)(2,1)S(1)}, bf16[64,2304]{1,0:T(8,128)(2,1)S(1)}, u32[]{:S(2)}, u32[]{:S(2)}) %collective-permute-start.1) | collective-permute-done | bytes 294944 | tf_op jit(solution)/shard_map/ppermute | solution.py:80
  24.2 1.5 %collective-permute-start.2 = (bf16[64,2304]{1,0:T(8,128)(2,1)S(1)}, bf16[64,2304]{1,0:T(8,128)(2,1)S(1)}, u32[]{:S(2)}, u32[]{:S(2)}) collective-permute-start(bf16[64,2304]{1,0:T(8,128)(2,1)S(1)} %collective-permute-done.1), channel_id=1, source_target_pairs={{0,8},{8,16},{16,24},{24,28},{28,20},{20,12},{12,4},{4,0},{1,9},{9... | collective-permute-start | bytes 884744 | tf_op jit(solution)/shard_map/ppermute | solution.py:80
  27.2 4.5 %collective-permute-done.2 = bf16[64,2304]{1,0:T(8,128)(2,1)S(1)} collective-permute-done((bf16[64,2304]{1,0:T(8,128)(2,1)S(1)}, bf16[64,2304]{1,0:T(8,128)(2,1)S(1)}, u32[]{:S(2)}, u32[]{:S(2)}) %collective-permute-start.2) | collective-permute-done | bytes 294944 | tf_op jit(solution)/shard_map/ppermute | solution.py:80
  31.8 1.3 %collective-permute-start.3 = (bf16[32,2304]{1,0:T(8,128)(2,1)S(1)}, bf16[32,2304]{1,0:T(8,128)(2,1)S(1)}, u32[]{:S(2)}, u32[]{:S(2)}) collective-permute-start(bf16[32,2304]{1,0:T(8,128)(2,1)S(1)} %slice.136), channel_id=1, source_target_pairs={{0,8},{8,16},{16,24},{24,28},{28,20},{20,12},{12,4},{4,0},{1,9},{9... | collective-permute-start | bytes 442376 | tf_op jit(solution)/shard_map/ppermute | solution.py:82
  34.4 2.6 %collective-permute-done.3 = bf16[32,2304]{1,0:T(8,128)(2,1)S(1)} collective-permute-done((bf16[32,2304]{1,0:T(8,128)(2,1)S(1)}, bf16[32,2304]{1,0:T(8,128)(2,1)S(1)}, u32[]{:S(2)}, u32[]{:S(2)}) %collective-permute-start.3) | collective-permute-done | bytes 147488 | tf_op jit(solution)/shard_map/ppermute | solution.py:82
  37.0 1.3 %collective-permute-done.7 = bf16[32,2304]{1,0:T(8,128)(2,1)S(1)} collective-permute-done((bf16[32,2304]{1,0:T(8,128)(2,1)S(1)}, bf16[32,2304]{1,0:T(8,128)(2,1)S(1)}, u32[]{:S(2)}, u32[]{:S(2)}) %collective-permute-start.7) | collective-permute-done | bytes 147488 | tf_op jit(solution)/shard_map/ppermute | solution.py:82
  41.2 1.6 %collective-permute-start.25 = (bf16[32,2304]{1,0:T(8,128)(2,1)S(1)}, bf16[32,2304]{1,0:T(8,128)(2,1)S(1)}, u32[]{:S(2)}, u32[]{:S(2)}) collective-permute-start(bf16[32,2304]{1,0:T(8,128)(2,1)S(1)} %get-tuple-element.29), channel_id=1, source_target_pairs={{0,8},{8,16},{16,24},{24,28},{28,20},{20,12},{12,4},{4,0},{1,9},{9... | collective-permute-start | bytes 442376 | tf_op jit(solution)/shard_map/ppermute | solution.py:122
  47.7 3.5 %collective-permute-start.22 = (bf16[192,2304]{1,0:T(8,128)(2,1)S(1)}, bf16[192,2304]{1,0:T(8,128)(2,1)S(1)}, u32[]{:S(2)}, u32[]{:S(2)}) collective-permute-start(bf16[192,2304]{1,0:T(8,128)(2,1)S(1)} %pad_maximum_fusion.3), channel_id=1, source_target_pairs={{0,2},{1,3},{4,6},{5,7},{8,10},{9,11},{12,14},{13,15},{16,18},{17,... | collective-permute-start | bytes 2654216 | tf_op jit(solution)/shard_map/ppermute | solution.py:112
  54.4 1.6 %collective-permute-start.30 = (bf16[32,2304]{1,0:T(8,128)(2,1)S(1)}, bf16[32,2304]{1,0:T(8,128)(2,1)S(1)}, u32[]{:S(2)}, u32[]{:S(2)}) collective-permute-start(bf16[32,2304]{1,0:T(8,128)(2,1)S(1)} %get-tuple-element.15), channel_id=1, source_target_pairs={{8,0},{16,8},{24,16},{28,24},{20,28},{12,20},{4,12},{0,4},{9,1},{1... | collective-permute-start | bytes 442376 | tf_op jit(solution)/shard_map/ppermute | solution.py:122
  56.5 1.6 %collective-permute-start.16 = (bf16[32,2304]{1,0:T(8,128)(2,1)S(1)}, bf16[32,2304]{1,0:T(8,128)(2,1)S(1)}, u32[]{:S(2)}, u32[]{:S(2)}) collective-permute-start(bf16[32,2304]{1,0:T(8,128)(2,1)S(1)} %get-tuple-element.42), channel_id=1, source_target_pairs={{8,0},{16,8},{24,16},{28,24},{20,28},{12,20},{4,12},{0,4},{9,1},{1... | collective-permute-start | bytes 442376 | tf_op jit(solution)/shard_map/ppermute | solution.py:122
  58.2 1.6 %collective-permute-done.33 = bf16[32,2304]{1,0:T(8,128)(2,1)S(1)} collective-permute-done((bf16[32,2304]{1,0:T(8,128)(2,1)S(1)}, bf16[32,2304]{1,0:T(8,128)(2,1)S(1)}, u32[]{:S(2)}, u32[]{:S(2)}) %collective-permute-start.33) | collective-permute-done | bytes 147488 | tf_op jit(solution)/shard_map/ppermute | solution.py:122
  59.7 1.6 %collective-permute-start.10 = (bf16[32,2304]{1,0:T(8,128)(2,1)S(1)}, bf16[32,2304]{1,0:T(8,128)(2,1)S(1)}, u32[]{:S(2)}, u32[]{:S(2)}) collective-permute-start(bf16[32,2304]{1,0:T(8,128)(2,1)S(1)} %get-tuple-element.38), channel_id=1, source_target_pairs={{0,8},{8,16},{16,24},{24,28},{28,20},{20,12},{12,4},{4,0},{1,9},{9... | collective-permute-start | bytes 442376 | tf_op jit(solution)/shard_map/ppermute | solution.py:122
  61.3 1.2 %collective-permute-done.14 = bf16[32,2304]{1,0:T(8,128)(2,1)S(1)} collective-permute-done((bf16[32,2304]{1,0:T(8,128)(2,1)S(1)}, bf16[32,2304]{1,0:T(8,128)(2,1)S(1)}, u32[]{:S(2)}, u32[]{:S(2)}) %collective-permute-start.14) | collective-permute-done | bytes 147488 | tf_op jit(solution)/shard_map/ppermute | solution.py:122
  63.2 1.0 collective-permute-done.16
  64.2 1.5 %collective-permute-start.27 = (bf16[64,2304]{1,0:T(8,128)(2,1)S(1)}, bf16[64,2304]{1,0:T(8,128)(2,1)S(1)}, u32[]{:S(2)}, u32[]{:S(2)}) collective-permute-start(bf16[64,2304]{1,0:T(8,128)(2,1)S(1)} %pad_maximum_fusion.5), channel_id=1, source_target_pairs={{0,2},{1,3},{4,6},{5,7},{8,10},{9,11},{12,14},{13,15},{16,18},{17,... | collective-permute-start | bytes 884744 | tf_op jit(solution)/shard_map/ppermute | solution.py:130
  65.8 1.6 %collective-permute-start.15 = (bf16[32,2304]{1,0:T(8,128)(2,1)S(1)}, bf16[32,2304]{1,0:T(8,128)(2,1)S(1)}, u32[]{:S(2)}, u32[]{:S(2)}) collective-permute-start(bf16[32,2304]{1,0:T(8,128)(2,1)S(1)} %add_convert_fusion.16), channel_id=1, source_target_pairs={{0,8},{8,16},{16,24},{24,28},{28,20},{20,12},{12,4},{4,0},{1,9},{9... | collective-permute-start | bytes 442376 | tf_op jit(solution)/shard_map/ppermute | solution.py:122
  67.5 3.5 %collective-permute-done.15 = bf16[32,2304]{1,0:T(8,128)(2,1)S(1)} collective-permute-done((bf16[32,2304]{1,0:T(8,128)(2,1)S(1)}, bf16[32,2304]{1,0:T(8,128)(2,1)S(1)}, u32[]{:S(2)}, u32[]{:S(2)}) %collective-permute-start.15) | collective-permute-done | bytes 147488 | tf_op jit(solution)/shard_map/ppermute | solution.py:122
  71.0 1.4 %collective-permute-start.17 = (bf16[32,2304]{1,0:T(8,128)(2,1)S(1)}, bf16[32,2304]{1,0:T(8,128)(2,1)S(1)}, u32[]{:S(2)}, u32[]{:S(2)}) collective-permute-start(bf16[32,2304]{1,0:T(8,128)(2,1)S(1)} %add_convert_fusion.14), channel_id=1, source_target_pairs={{8,0},{16,8},{24,16},{28,24},{20,28},{12,20},{4,12},{0,4},{9,1},{1... | collective-permute-start | bytes 442376 | tf_op jit(solution)/shard_map/ppermute | solution.py:122
  72.5 4.1 %collective-permute-done.17 = bf16[32,2304]{1,0:T(8,128)(2,1)S(1)} collective-permute-done((bf16[32,2304]{1,0:T(8,128)(2,1)S(1)}, bf16[32,2304]{1,0:T(8,128)(2,1)S(1)}, u32[]{:S(2)}, u32[]{:S(2)}) %collective-permute-start.17) | collective-permute-done | bytes 147488 | tf_op jit(solution)/shard_map/ppermute | solution.py:122
  77.7 1.6 %collective-permute-start.12 = (bf16[32,2304]{1,0:T(8,128)(2,1)S(1)}, bf16[32,2304]{1,0:T(8,128)(2,1)S(1)}, u32[]{:S(2)}, u32[]{:S(2)}) collective-permute-start(bf16[32,2304]{1,0:T(8,128)(2,1)S(1)} %add_convert_fusion.17), channel_id=1, source_target_pairs={{0,8},{8,16},{16,24},{24,28},{28,20},{20,12},{12,4},{4,0},{1,9},{9... | collective-permute-start | bytes 442376 | tf_op jit(solution)/shard_map/ppermute | solution.py:122
  79.3 2.7 %collective-permute-start.18 = (bf16[64,2304]{1,0:T(8,128)(2,1)S(1)}, bf16[64,2304]{1,0:T(8,128)(2,1)S(1)}, u32[]{:S(2)}, u32[]{:S(2)}) collective-permute-start(bf16[64,2304]{1,0:T(8,128)(2,1)S(1)} %pad_maximum_fusion.4), channel_id=1, source_target_pairs={{0,2},{1,3},{4,6},{5,7},{8,10},{9,11},{12,14},{13,15},{16,18},{17,... | collective-permute-start | bytes 884744 | tf_op jit(solution)/shard_map/ppermute | solution.py:130
  82.6 4.1 %collective-permute-done.18 = bf16[64,2304]{1,0:T(8,128)(2,1)S(1)} collective-permute-done((bf16[64,2304]{1,0:T(8,128)(2,1)S(1)}, bf16[64,2304]{1,0:T(8,128)(2,1)S(1)}, u32[]{:S(2)}, u32[]{:S(2)}) %collective-permute-start.18) | collective-permute-done | bytes 294944 | tf_op jit(solution)/shard_map/ppermute | solution.py:130
  86.7 1.6 %collective-permute-start.28 = (bf16[32,2304]{1,0:T(8,128)(2,1)S(1)}, bf16[32,2304]{1,0:T(8,128)(2,1)S(1)}, u32[]{:S(2)}, u32[]{:S(2)}) collective-permute-start(bf16[32,2304]{1,0:T(8,128)(2,1)S(1)} %add_convert_fusion.8), channel_id=1, source_target_pairs={{0,8},{8,16},{16,24},{24,28},{28,20},{20,12},{12,4},{4,0},{1,9},{9... | collective-permute-start | bytes 442376 | tf_op jit(solution)/shard_map/ppermute | solution.py:122
  88.9 1.6 %collective-permute-start.19 = (bf16[32,2304]{1,0:T(8,128)(2,1)S(1)}, bf16[32,2304]{1,0:T(8,128)(2,1)S(1)}, u32[]{:S(2)}, u32[]{:S(2)}) collective-permute-start(bf16[32,2304]{1,0:T(8,128)(2,1)S(1)} %add_convert_fusion.12), channel_id=1, source_target_pairs={{0,8},{8,16},{16,24},{24,28},{28,20},{20,12},{12,4},{4,0},{1,9},{9... | collective-permute-start | bytes 442376 | tf_op jit(solution)/shard_map/ppermute | solution.py:122
  91.3 3.5 %collective-permute-done.35 = bf16[32,2304]{1,0:T(8,128)(2,1)S(1)} collective-permute-done((bf16[32,2304]{1,0:T(8,128)(2,1)S(1)}, bf16[32,2304]{1,0:T(8,128)(2,1)S(1)}, u32[]{:S(2)}, u32[]{:S(2)}) %collective-permute-start.35) | collective-permute-done | bytes 147488 | tf_op jit(solution)/shard_map/ppermute | solution.py:122
  95.7 1.6 %collective-permute-start.23 = (bf16[32,2304]{1,0:T(8,128)(2,1)S(1)}, bf16[32,2304]{1,0:T(8,128)(2,1)S(1)}, u32[]{:S(2)}, u32[]{:S(2)}) collective-permute-start(bf16[32,2304]{1,0:T(8,128)(2,1)S(1)} %add_convert_fusion.11), channel_id=1, source_target_pairs={{0,8},{8,16},{16,24},{24,28},{28,20},{20,12},{12,4},{4,0},{1,9},{9... | collective-permute-start | bytes 442376 | tf_op jit(solution)/shard_map/ppermute | solution.py:122
  97.4 1.6 %collective-permute-start.29 = (bf16[32,2304]{1,0:T(8,128)(2,1)S(1)}, bf16[32,2304]{1,0:T(8,128)(2,1)S(1)}, u32[]{:S(2)}, u32[]{:S(2)}) collective-permute-start(bf16[32,2304]{1,0:T(8,128)(2,1)S(1)} %add_convert_fusion.7), channel_id=1, source_target_pairs={{0,8},{8,16},{16,24},{24,28},{28,20},{20,12},{12,4},{4,0},{1,9},{9... | collective-permute-start | bytes 442376 | tf_op jit(solution)/shard_map/ppermute | solution.py:122
  100.9 1.7 %collective-permute-done.29 = bf16[32,2304]{1,0:T(8,128)(2,1)S(1)} collective-permute-done((bf16[32,2304]{1,0:T(8,128)(2,1)S(1)}, bf16[32,2304]{1,0:T(8,128)(2,1)S(1)}, u32[]{:S(2)}, u32[]{:S(2)}) %collective-permute-start.29) | collective-permute-done | bytes 147488 | tf_op jit(solution)/shard_map/ppermute | solution.py:122
  (104 shorter events, 23.8 us)
Async XLA Ops:
  5.0 33.8 %collective-permute-start.9 = (bf16[2,512,2304]{2,1,0:T(8,128)(2,1)S(1)}, bf16[2,512,2304]{2,1,0:T(8,128)(2,1)S(1)}, u32[]{:S(2)}, u32[]{:S(2)}) collective-permute-start(bf16[2,512,2304]{2,1,0:T(8,128)(2,1)S(1)} %pad_maximum_fusion), channel_id=1, source_target_pairs={{0,1},{1,0},{2,3},{3,2},{4,5},{5,4},{6,7},{7,6},{8,9},{9,8},{10,11... | collective-permute-start | bytes 14155784 | tf_op jit(solution)/shard_map/ppermute | solution.py:72
  5.6 10.2 %collective-permute-start = (bf16[64,2304]{1,0:T(8,128)(2,1)S(1)}, bf16[64,2304]{1,0:T(8,128)(2,1)S(1)}, u32[]{:S(2)}, u32[]{:S(2)}) collective-permute-start(bf16[64,2304]{1,0:T(8,128)(2,1)S(1)} %bitcast.69), channel_id=1, source_target_pairs={{0,8},{8,16},{16,24},{24,28},{28,20},{20,12},{12,4},{4,0},{1,9},{9... | collective-permute-start | bytes 884744 | tf_op jit(solution)/shard_map/ppermute | solution.py:80
  8.5 9.0 %collective-permute-start.4 = (bf16[64,2304]{1,0:T(8,128)(2,1)S(1)}, bf16[64,2304]{1,0:T(8,128)(2,1)S(1)}, u32[]{:S(2)}, u32[]{:S(2)}) collective-permute-start(bf16[64,2304]{1,0:T(8,128)(2,1)S(1)} %bitcast.70), channel_id=1, source_target_pairs={{8,0},{16,8},{24,16},{28,24},{20,28},{12,20},{4,12},{0,4},{9,1},{1... | collective-permute-start | bytes 884744 | tf_op jit(solution)/shard_map/ppermute | solution.py:81
  15.7 8.4 %collective-permute-start.1 = (bf16[64,2304]{1,0:T(8,128)(2,1)S(1)}, bf16[64,2304]{1,0:T(8,128)(2,1)S(1)}, u32[]{:S(2)}, u32[]{:S(2)}) collective-permute-start(bf16[64,2304]{1,0:T(8,128)(2,1)S(1)} %collective-permute-done), channel_id=1, source_target_pairs={{0,8},{8,16},{16,24},{24,28},{28,20},{20,12},{12,4},{4,0},{1,9},{9... | collective-permute-start | bytes 884744 | tf_op jit(solution)/shard_map/ppermute | solution.py:80
  17.5 8.1 %collective-permute-start.5 = (bf16[64,2304]{1,0:T(8,128)(2,1)S(1)}, bf16[64,2304]{1,0:T(8,128)(2,1)S(1)}, u32[]{:S(2)}, u32[]{:S(2)}) collective-permute-start(bf16[64,2304]{1,0:T(8,128)(2,1)S(1)} %collective-permute-done.4), channel_id=1, source_target_pairs={{8,0},{16,8},{24,16},{28,24},{20,28},{12,20},{4,12},{0,4},{9,1},{1... | collective-permute-start | bytes 884744 | tf_op jit(solution)/shard_map/ppermute | solution.py:81
  18.3 28.4 %collective-permute-start.21 = (bf16[64,512]{1,0:T(8,128)(2,1)S(1)}, bf16[64,512]{1,0:T(8,128)(2,1)S(1)}, u32[]{:S(2)}, u32[]{:S(2)}) collective-permute-start(bf16[64,512]{1,0:T(8,128)(2,1)S(1)} %fusion.49), channel_id=1, source_target_pairs={{0,1},{1,0},{2,3},{3,2},{4,5},{5,4},{6,7},{7,6},{8,9},{9,8},{10,11... | collective-permute-start | bytes 196616 | tf_op jit(solution)/shard_map/ppermute | solution.py:89
  24.2 7.6 %collective-permute-start.2 = (bf16[64,2304]{1,0:T(8,128)(2,1)S(1)}, bf16[64,2304]{1,0:T(8,128)(2,1)S(1)}, u32[]{:S(2)}, u32[]{:S(2)}) collective-permute-start(bf16[64,2304]{1,0:T(8,128)(2,1)S(1)} %collective-permute-done.1), channel_id=1, source_target_pairs={{0,8},{8,16},{16,24},{24,28},{28,20},{20,12},{12,4},{4,0},{1,9},{9... | collective-permute-start | bytes 884744 | tf_op jit(solution)/shard_map/ppermute | solution.py:80
  25.7 7.4 %collective-permute-start.6 = (bf16[64,2304]{1,0:T(8,128)(2,1)S(1)}, bf16[64,2304]{1,0:T(8,128)(2,1)S(1)}, u32[]{:S(2)}, u32[]{:S(2)}) collective-permute-start(bf16[64,2304]{1,0:T(8,128)(2,1)S(1)} %collective-permute-done.5), channel_id=1, source_target_pairs={{8,0},{16,8},{24,16},{28,24},{20,28},{12,20},{4,12},{0,4},{9,1},{1... | collective-permute-start | bytes 884744 | tf_op jit(solution)/shard_map/ppermute | solution.py:81
  26.7 19.2 %collective-permute-start.20 = (bf16[128,512]{1,0:T(8,128)(2,1)S(1)}, bf16[128,512]{1,0:T(8,128)(2,1)S(1)}, u32[]{:S(2)}, u32[]{:S(2)}) collective-permute-start(bf16[128,512]{1,0:T(8,128)(2,1)S(1)} %fusion.34), channel_id=1, source_target_pairs={{0,1},{1,0},{2,3},{3,2},{4,5},{5,4},{6,7},{7,6},{8,9},{9,8},{10,11... | collective-permute-start | bytes 393224 | tf_op jit(solution)/shard_map/ppermute | solution.py:89
  31.8 5.2 %collective-permute-start.3 = (bf16[32,2304]{1,0:T(8,128)(2,1)S(1)}, bf16[32,2304]{1,0:T(8,128)(2,1)S(1)}, u32[]{:S(2)}, u32[]{:S(2)}) collective-permute-start(bf16[32,2304]{1,0:T(8,128)(2,1)S(1)} %slice.136), channel_id=1, source_target_pairs={{0,8},{8,16},{16,24},{24,28},{28,20},{20,12},{12,4},{4,0},{1,9},{9... | collective-permute-start | bytes 442376 | tf_op jit(solution)/shard_map/ppermute | solution.py:82
  36.9 5.9 %collective-permute-start.13 = (bf16[128,512]{1,0:T(8,128)(2,1)S(1)}, bf16[128,512]{1,0:T(8,128)(2,1)S(1)}, u32[]{:S(2)}, u32[]{:S(2)}) collective-permute-start(bf16[128,512]{1,0:T(8,128)(2,1)S(1)} %fusion.31), channel_id=1, source_target_pairs={{0,1},{1,0},{2,3},{3,2},{4,5},{5,4},{6,7},{7,6},{8,9},{9,8},{10,11... | collective-permute-start | bytes 393224 | tf_op jit(solution)/shard_map/ppermute | solution.py:89
  38.8 13.2 %collective-permute-start.8 = (bf16[64,512]{1,0:T(8,128)(2,1)S(1)}, bf16[64,512]{1,0:T(8,128)(2,1)S(1)}, u32[]{:S(2)}, u32[]{:S(2)}) collective-permute-start(bf16[64,512]{1,0:T(8,128)(2,1)S(1)} %fusion.52), channel_id=1, source_target_pairs={{0,1},{1,0},{2,3},{3,2},{4,5},{5,4},{6,7},{7,6},{8,9},{9,8},{10,11... | collective-permute-start | bytes 196616 | tf_op jit(solution)/shard_map/ppermute | solution.py:89
  41.2 14.8 %collective-permute-start.25 = (bf16[32,2304]{1,0:T(8,128)(2,1)S(1)}, bf16[32,2304]{1,0:T(8,128)(2,1)S(1)}, u32[]{:S(2)}, u32[]{:S(2)}) collective-permute-start(bf16[32,2304]{1,0:T(8,128)(2,1)S(1)} %get-tuple-element.29), channel_id=1, source_target_pairs={{0,8},{8,16},{16,24},{24,28},{28,20},{20,12},{12,4},{4,0},{1,9},{9... | collective-permute-start | bytes 442376 | tf_op jit(solution)/shard_map/ppermute | solution.py:122
  43.7 12.9 %collective-permute-start.26 = (bf16[32,2304]{1,0:T(8,128)(2,1)S(1)}, bf16[32,2304]{1,0:T(8,128)(2,1)S(1)}, u32[]{:S(2)}, u32[]{:S(2)}) collective-permute-start(bf16[32,2304]{1,0:T(8,128)(2,1)S(1)} %get-tuple-element.28), channel_id=1, source_target_pairs={{8,0},{16,8},{24,16},{28,24},{20,28},{12,20},{4,12},{0,4},{9,1},{1... | collective-permute-start | bytes 442376 | tf_op jit(solution)/shard_map/ppermute | solution.py:122
  47.7 42.8 %collective-permute-start.22 = (bf16[192,2304]{1,0:T(8,128)(2,1)S(1)}, bf16[192,2304]{1,0:T(8,128)(2,1)S(1)}, u32[]{:S(2)}, u32[]{:S(2)}) collective-permute-start(bf16[192,2304]{1,0:T(8,128)(2,1)S(1)} %pad_maximum_fusion.3), channel_id=1, source_target_pairs={{0,2},{1,3},{4,6},{5,7},{8,10},{9,11},{12,14},{13,15},{16,18},{17,... | collective-permute-start | bytes 2654216 | tf_op jit(solution)/shard_map/ppermute | solution.py:112
  52.9 6.8 %collective-permute-start.33 = (bf16[32,2304]{1,0:T(8,128)(2,1)S(1)}, bf16[32,2304]{1,0:T(8,128)(2,1)S(1)}, u32[]{:S(2)}, u32[]{:S(2)}) collective-permute-start(bf16[32,2304]{1,0:T(8,128)(2,1)S(1)} %get-tuple-element.37), channel_id=1, source_target_pairs={{8,0},{16,8},{24,16},{28,24},{20,28},{12,20},{4,12},{0,4},{9,1},{1... | collective-permute-start | bytes 442376 | tf_op jit(solution)/shard_map/ppermute | solution.py:122
  54.4 24.9 %collective-permute-start.30 = (bf16[32,2304]{1,0:T(8,128)(2,1)S(1)}, bf16[32,2304]{1,0:T(8,128)(2,1)S(1)}, u32[]{:S(2)}, u32[]{:S(2)}) collective-permute-start(bf16[32,2304]{1,0:T(8,128)(2,1)S(1)} %get-tuple-element.15), channel_id=1, source_target_pairs={{8,0},{16,8},{24,16},{28,24},{20,28},{12,20},{4,12},{0,4},{9,1},{1... | collective-permute-start | bytes 442376 | tf_op jit(solution)/shard_map/ppermute | solution.py:122
  56.0 6.6 %collective-permute-start.14 = (bf16[32,2304]{1,0:T(8,128)(2,1)S(1)}, bf16[32,2304]{1,0:T(8,128)(2,1)S(1)}, u32[]{:S(2)}, u32[]{:S(2)}) collective-permute-start(bf16[32,2304]{1,0:T(8,128)(2,1)S(1)} %get-tuple-element.41), channel_id=1, source_target_pairs={{0,8},{8,16},{16,24},{24,28},{28,20},{20,12},{12,4},{4,0},{1,9},{9... | collective-permute-start | bytes 442376 | tf_op jit(solution)/shard_map/ppermute | solution.py:122
  56.5 7.7 %collective-permute-start.16 = (bf16[32,2304]{1,0:T(8,128)(2,1)S(1)}, bf16[32,2304]{1,0:T(8,128)(2,1)S(1)}, u32[]{:S(2)}, u32[]{:S(2)}) collective-permute-start(bf16[32,2304]{1,0:T(8,128)(2,1)S(1)} %get-tuple-element.42), channel_id=1, source_target_pairs={{8,0},{16,8},{24,16},{28,24},{20,28},{12,20},{4,12},{0,4},{9,1},{1... | collective-permute-start | bytes 442376 | tf_op jit(solution)/shard_map/ppermute | solution.py:122
  59.7 6.1 %collective-permute-start.10 = (bf16[32,2304]{1,0:T(8,128)(2,1)S(1)}, bf16[32,2304]{1,0:T(8,128)(2,1)S(1)}, u32[]{:S(2)}, u32[]{:S(2)}) collective-permute-start(bf16[32,2304]{1,0:T(8,128)(2,1)S(1)} %get-tuple-element.38), channel_id=1, source_target_pairs={{0,8},{8,16},{16,24},{24,28},{28,20},{20,12},{12,4},{4,0},{1,9},{9... | collective-permute-start | bytes 442376 | tf_op jit(solution)/shard_map/ppermute | solution.py:122
  62.6 19.5 %collective-permute-start.24 = (bf16[32,2304]{1,0:T(8,128)(2,1)S(1)}, bf16[32,2304]{1,0:T(8,128)(2,1)S(1)}, u32[]{:S(2)}, u32[]{:S(2)}) collective-permute-start(bf16[32,2304]{1,0:T(8,128)(2,1)S(1)} %get-tuple-element.17), channel_id=1, source_target_pairs={{0,8},{8,16},{16,24},{24,28},{28,20},{20,12},{12,4},{4,0},{1,9},{9... | collective-permute-start | bytes 442376 | tf_op jit(solution)/shard_map/ppermute | solution.py:122
  64.2 13.4 %collective-permute-start.27 = (bf16[64,2304]{1,0:T(8,128)(2,1)S(1)}, bf16[64,2304]{1,0:T(8,128)(2,1)S(1)}, u32[]{:S(2)}, u32[]{:S(2)}) collective-permute-start(bf16[64,2304]{1,0:T(8,128)(2,1)S(1)} %pad_maximum_fusion.5), channel_id=1, source_target_pairs={{0,2},{1,3},{4,6},{5,7},{8,10},{9,11},{12,14},{13,15},{16,18},{17,... | collective-permute-start | bytes 884744 | tf_op jit(solution)/shard_map/ppermute | solution.py:130
  71.0 5.6 %collective-permute-start.17 = (bf16[32,2304]{1,0:T(8,128)(2,1)S(1)}, bf16[32,2304]{1,0:T(8,128)(2,1)S(1)}, u32[]{:S(2)}, u32[]{:S(2)}) collective-permute-start(bf16[32,2304]{1,0:T(8,128)(2,1)S(1)} %add_convert_fusion.14), channel_id=1, source_target_pairs={{8,0},{16,8},{24,16},{28,24},{20,28},{12,20},{4,12},{0,4},{9,1},{1... | collective-permute-start | bytes 442376 | tf_op jit(solution)/shard_map/ppermute | solution.py:122
  76.6 11.7 %collective-permute-start.34 = (bf16[32,2304]{1,0:T(8,128)(2,1)S(1)}, bf16[32,2304]{1,0:T(8,128)(2,1)S(1)}, u32[]{:S(2)}, u32[]{:S(2)}) collective-permute-start(bf16[32,2304]{1,0:T(8,128)(2,1)S(1)} %add_convert_fusion.4), channel_id=1, source_target_pairs={{8,0},{16,8},{24,16},{28,24},{20,28},{12,20},{4,12},{0,4},{9,1},{1... | collective-permute-start | bytes 442376 | tf_op jit(solution)/shard_map/ppermute | solution.py:122
  77.7 11.2 %collective-permute-start.12 = (bf16[32,2304]{1,0:T(8,128)(2,1)S(1)}, bf16[32,2304]{1,0:T(8,128)(2,1)S(1)}, u32[]{:S(2)}, u32[]{:S(2)}) collective-permute-start(bf16[32,2304]{1,0:T(8,128)(2,1)S(1)} %add_convert_fusion.17), channel_id=1, source_target_pairs={{0,8},{8,16},{16,24},{24,28},{28,20},{20,12},{12,4},{4,0},{1,9},{9... | collective-permute-start | bytes 442376 | tf_op jit(solution)/shard_map/ppermute | solution.py:122
  79.3 7.4 %collective-permute-start.18 = (bf16[64,2304]{1,0:T(8,128)(2,1)S(1)}, bf16[64,2304]{1,0:T(8,128)(2,1)S(1)}, u32[]{:S(2)}, u32[]{:S(2)}) collective-permute-start(bf16[64,2304]{1,0:T(8,128)(2,1)S(1)} %pad_maximum_fusion.4), channel_id=1, source_target_pairs={{0,2},{1,3},{4,6},{5,7},{8,10},{9,11},{12,14},{13,15},{16,18},{17,... | collective-permute-start | bytes 884744 | tf_op jit(solution)/shard_map/ppermute | solution.py:130
  82.0 8.7 %collective-permute-start.31 = (bf16[32,2304]{1,0:T(8,128)(2,1)S(1)}, bf16[32,2304]{1,0:T(8,128)(2,1)S(1)}, u32[]{:S(2)}, u32[]{:S(2)}) collective-permute-start(bf16[32,2304]{1,0:T(8,128)(2,1)S(1)} %add_convert_fusion.6), channel_id=1, source_target_pairs={{8,0},{16,8},{24,16},{28,24},{20,28},{12,20},{4,12},{0,4},{9,1},{1... | collective-permute-start | bytes 442376 | tf_op jit(solution)/shard_map/ppermute | solution.py:122
  86.7 10.7 %collective-permute-start.28 = (bf16[32,2304]{1,0:T(8,128)(2,1)S(1)}, bf16[32,2304]{1,0:T(8,128)(2,1)S(1)}, u32[]{:S(2)}, u32[]{:S(2)}) collective-permute-start(bf16[32,2304]{1,0:T(8,128)(2,1)S(1)} %add_convert_fusion.8), channel_id=1, source_target_pairs={{0,8},{8,16},{16,24},{24,28},{28,20},{20,12},{12,4},{4,0},{1,9},{9... | collective-permute-start | bytes 442376 | tf_op jit(solution)/shard_map/ppermute | solution.py:122
  88.4 6.5 %collective-permute-start.35 = (bf16[32,2304]{1,0:T(8,128)(2,1)S(1)}, bf16[32,2304]{1,0:T(8,128)(2,1)S(1)}, u32[]{:S(2)}, u32[]{:S(2)}) collective-permute-start(bf16[32,2304]{1,0:T(8,128)(2,1)S(1)} %add_convert_fusion.3), channel_id=1, source_target_pairs={{8,0},{16,8},{24,16},{28,24},{20,28},{12,20},{4,12},{0,4},{9,1},{1... | collective-permute-start | bytes 442376 | tf_op jit(solution)/shard_map/ppermute | solution.py:122
  88.9 6.7 %collective-permute-start.19 = (bf16[32,2304]{1,0:T(8,128)(2,1)S(1)}, bf16[32,2304]{1,0:T(8,128)(2,1)S(1)}, u32[]{:S(2)}, u32[]{:S(2)}) collective-permute-start(bf16[32,2304]{1,0:T(8,128)(2,1)S(1)} %add_convert_fusion.12), channel_id=1, source_target_pairs={{0,8},{8,16},{16,24},{24,28},{28,20},{20,12},{12,4},{4,0},{1,9},{9... | collective-permute-start | bytes 442376 | tf_op jit(solution)/shard_map/ppermute | solution.py:122
  90.8 9.1 %collective-permute-start.32 = (bf16[32,2304]{1,0:T(8,128)(2,1)S(1)}, bf16[32,2304]{1,0:T(8,128)(2,1)S(1)}, u32[]{:S(2)}, u32[]{:S(2)}) collective-permute-start(bf16[32,2304]{1,0:T(8,128)(2,1)S(1)} %add_convert_fusion.5), channel_id=1, source_target_pairs={{8,0},{16,8},{24,16},{28,24},{20,28},{12,20},{4,12},{0,4},{9,1},{1... | collective-permute-start | bytes 442376 | tf_op jit(solution)/shard_map/ppermute | solution.py:122
  95.7 5.2 %collective-permute-start.23 = (bf16[32,2304]{1,0:T(8,128)(2,1)S(1)}, bf16[32,2304]{1,0:T(8,128)(2,1)S(1)}, u32[]{:S(2)}, u32[]{:S(2)}) collective-permute-start(bf16[32,2304]{1,0:T(8,128)(2,1)S(1)} %add_convert_fusion.11), channel_id=1, source_target_pairs={{0,8},{8,16},{16,24},{24,28},{28,20},{20,12},{12,4},{4,0},{1,9},{9... | collective-permute-start | bytes 442376 | tf_op jit(solution)/shard_map/ppermute | solution.py:122
  (10 other events, 74.5 us)

commit v3 on v2

--- a/solution.py
+++ b/solution.py
@@ -74,13 +74,14 @@
     upper = jnp.concatenate([decoder(dec_weight, 2 + core), take[1]], axis=0)
     near, upper = lax.optimization_barrier((near, upper))
 
-    fwd = [rows]
-    bwd = [rows]
-    for _ in range(1, far):
-        fwd.append(lax.ppermute(fwd[-1], "feat", ahead))
-        bwd.append(lax.ppermute(bwd[-1], "feat", back))
-    ends = [lax.ppermute(fwd[-1][:half], "feat", ahead), lax.ppermute(bwd[-1][half:], "feat", back)]
-    chunks = [rows] + [jnp.concatenate([bwd[d], fwd[d]], axis=0) for d in range(1, far)] + [jnp.concatenate(ends, axis=0)]
+    fwd = [(rows,), (lax.ppermute(rows, "feat", ahead),)]
+    bwd = [(rows,), (lax.ppermute(rows, "feat", back),)]
+    for _ in range(2, far):
+        for line, pairs in ((fwd, ahead), (bwd, back)):
+            parts = line[-1] if len(line[-1]) > 1 else (line[-1][0][:half], line[-1][0][half:])
+            line.append(tuple(lax.ppermute(parts[i], "feat", pairs) for i in (0, 1)))
+    ends = [lax.ppermute(fwd[-1][0], "feat", ahead), lax.ppermute(bwd[-1][1], "feat", back)]
+    chunks = [rows] + [jnp.concatenate(bwd[d] + fwd[d], axis=0) for d in range(1, far)] + [jnp.concatenate(ends, axis=0)]
 
     made = []
     for chunk in chunks:
@@ -109,9 +110,9 @@
     ways = [(True, 0), (True, 1), (False, 0), (False, 1)]
     begins = {w: far if w[0] == (w[1] == 0) else far - 1 for w in ways}
 
-    got = lax.ppermute(jnp.concatenate([made[1][1], made[0][1]], axis=0), "layer", over)
-    straight = got[2 * count :]
-    made[1][0] = lax.optimization_barrier(plus(made[1][0], got[: 2 * count]))
+    got = lax.ppermute(made[1][1], "layer", over)
+    straight = lax.ppermute(made[0][1], "layer", over)
+    made[1][0] = lax.optimization_barrier(plus(made[1][0], got))
 
     crossed = {}
 

time: 104 us -> 114 us (1.096)
  starting transfers between devices: 40.5 us -> 50.6 us
    ppermute x9 -> x14, starting transfers between devices: 12.6 us -> 19.6 us  [the longest x8 8.89 us: ring_form(): line.append(tuple((lax.ppermute(parts[i], 'feat', pairs) for i in (0, 1))))]
    ppermute x9 -> x14, waiting for transfers between devices: 21.3 us -> 16.7 us  [the longest x1 6.61 us: ring_form(): fwd = [(rows,), (lax.ppermute(rows, 'feat', ahead),)]]
    ppermute x20, waiting for transfers between devices: 18 us -> 22.4 us  [chain(): got = lax.ppermute(value, 'feat', ahead if forward else back)]
    ppermute x2, starting transfers between devices: 4.18 us -> 5.95 us  [ring_form(): lax.ppermute(jnp.concatenate([chain(1, w, CROSS) for w in pair], axis=0),...]
  transfers between devices with their start and end apart: 37 -> 42, of which waited for: 16 -> 20; matrix products, arithmetic and copies ran while one was open for 13% -> 12% of each run, Pallas kernels for 0% -> 0%
where the time goes in v3:
time: 114 us; the launch traced here: 113 us
  starting transfers between devices  50.6 us (44%)
  waiting for transfers between devices  43.3 us (38%)
  matrix products  10.9 us (10%)
  other arithmetic  7.44 us (7%)
    ppermute x20, starting transfers between devices, chain(): got = lax.ppermute(value, 'feat', ahead if forward else back)  23.4 us
    ppermute x20, waiting for transfers between devices, chain(): got = lax.ppermute(value, 'feat', ahead if forward else back)  22.4 us
    ppermute x8, starting transfers between devices, ring_form(): line.append(tuple((lax.ppermute(parts[i], 'feat', pairs) for i in (0, 1))))  8.89 us
    dot_general x10, matrix products, ring_form(): jnp.dot(both, w, preferred_element_type=jnp.float32).astype(jnp.bfloat16)  8.44 us
    ppermute x1, waiting for transfers between devices, ring_form(): fwd = [(rows,), (lax.ppermute(rows, 'feat', ahead),)]  6.61 us
    ppermute x8, waiting for transfers between devices, ring_form(): line.append(tuple((lax.ppermute(parts[i], 'feat', pairs) for i in (0, 1))))  6.6 us
    ppermute x2, starting transfers between devices, ring_form(): lax.ppermute(jnp.concatenate([chain(1, w, CROSS) for w in pair], axis=0),...  5.95 us
    squeeze x1, other arithmetic, decoder(): return lax.dynamic_index_in_dim(weights[0], target, 0, keepdims=False)  4.52 us
  transfers between devices with their start and end apart: 42, of which 20 were waited for; matrix products, arithmetic and copies ran while one was open for 12% of the time, Pallas kernels for 0%

profile of v3, /device:TPU:0, one launch (start us, length us, event | category | flops | bytes accessed | tf_op | source)
XLA Modules:
  0.0 113.4 jit_solution(3867784542574873293)
XLA Ops:
  0.0 4.5 %dynamic-slice_bitcast_fusion = (bf16[512,2304]{1,0:T(8,128)(2,1)S(1)}, bf16[1,512,2304]{2,1,0:T(8,128)(2,1)S(1)}, bf16[512,2304]{1,0:T(8,128)(2,1)S(1)}, bf16[1,512,2304]{2,1,0:T(8,128)(2,1)S(1)}) fusion(bf16[1,4,512,2304]{3,2,1,0:T(8,128)(2,1)} %param.8, s32[]{:T(128)S(6)} %select_n.45, s32[]{:T(128)S(6)} %select_n.41, pred[]{:T(512)S(6)} %eq.5, ...), kind=kLoop, calls=%fused_computation.25 | loop fusion | flops 1179648 | bytes 18874384 | tf_op jit(solution)/shard_map/jit(dynamic_index_in_dim)/squeeze | solution.py:68
  5.6 3.0 %collective-permute-start = (bf16[64,2304]{1,0:T(8,128)(2,1)S(1)}, bf16[64,2304]{1,0:T(8,128)(2,1)S(1)}, u32[]{:S(2)}, u32[]{:S(2)}) collective-permute-start(bf16[64,2304]{1,0:T(8,128)(2,1)S(1)} %bitcast.69), channel_id=1, source_target_pairs={{0,8},{8,16},{16,24},{24,28},{28,20},{20,12},{12,4},{4,0},{1,9},{9... | collective-permute-start | bytes 884744 | tf_op jit(solution)/shard_map/ppermute | solution.py:77
  9.1 6.6 %collective-permute-done = bf16[64,2304]{1,0:T(8,128)(2,1)S(1)} collective-permute-done((bf16[64,2304]{1,0:T(8,128)(2,1)S(1)}, bf16[64,2304]{1,0:T(8,128)(2,1)S(1)}, u32[]{:S(2)}, u32[]{:S(2)}) %collective-permute-start) | collective-permute-done | bytes 294944 | tf_op jit(solution)/shard_map/ppermute | solution.py:77
  15.8 1.9 %collective-permute-start.1 = (bf16[32,2304]{1,0:T(8,128)(2,1)S(1)}, bf16[32,2304]{1,0:T(8,128)(2,1)S(1)}, u32[]{:S(2)}, u32[]{:S(2)}) collective-permute-start(bf16[32,2304]{1,0:T(8,128)(2,1)S(1)} %get-tuple-element.45), channel_id=1, source_target_pairs={{0,8},{8,16},{16,24},{24,28},{28,20},{20,12},{12,4},{4,0},{1,9},{9... | collective-permute-start | bytes 442376 | tf_op jit(solution)/shard_map/ppermute | solution.py:82
  17.9 1.7 %collective-permute-start.11 = (bf16[32,2304]{1,0:T(8,128)(2,1)S(1)}, bf16[32,2304]{1,0:T(8,128)(2,1)S(1)}, u32[]{:S(2)}, u32[]{:S(2)}) collective-permute-start(bf16[32,2304]{1,0:T(8,128)(2,1)S(1)} %get-tuple-element.43), channel_id=1, source_target_pairs={{8,0},{16,8},{24,16},{28,24},{20,28},{12,20},{4,12},{0,4},{9,1},{1... | collective-permute-start | bytes 442376 | tf_op jit(solution)/shard_map/ppermute | solution.py:82
  21.8 2.5 %collective-permute-start.2 = (bf16[32,2304]{1,0:T(8,128)(2,1)S(1)}, bf16[32,2304]{1,0:T(8,128)(2,1)S(1)}, u32[]{:S(2)}, u32[]{:S(2)}) collective-permute-start(bf16[32,2304]{1,0:T(8,128)(2,1)S(1)} %collective-permute-done.1), channel_id=1, source_target_pairs={{0,8},{8,16},{16,24},{24,28},{28,20},{20,12},{12,4},{4,0},{1,9},{9... | collective-permute-start | bytes 442376 | tf_op jit(solution)/shard_map/ppermute | solution.py:82
  24.6 2.9 %collective-permute-done.11 = bf16[32,2304]{1,0:T(8,128)(2,1)S(1)} collective-permute-done((bf16[32,2304]{1,0:T(8,128)(2,1)S(1)}, bf16[32,2304]{1,0:T(8,128)(2,1)S(1)}, u32[]{:S(2)}, u32[]{:S(2)}) %collective-permute-start.11) | collective-permute-done | bytes 147488 | tf_op jit(solution)/shard_map/ppermute | solution.py:82
  27.8 1.8 %collective-permute-start.14 = (bf16[32,2304]{1,0:T(8,128)(2,1)S(1)}, bf16[32,2304]{1,0:T(8,128)(2,1)S(1)}, u32[]{:S(2)}, u32[]{:S(2)}) collective-permute-start(bf16[32,2304]{1,0:T(8,128)(2,1)S(1)} %collective-permute-done.13), channel_id=1, source_target_pairs={{0,8},{8,16},{16,24},{24,28},{28,20},{20,12},{12,4},{4,0},{1,9},{9... | collective-permute-start | bytes 442376 | tf_op jit(solution)/shard_map/ppermute | solution.py:82
  30.7 2.0 %collective-permute-done.12 = bf16[32,2304]{1,0:T(8,128)(2,1)S(1)} collective-permute-done((bf16[32,2304]{1,0:T(8,128)(2,1)S(1)}, bf16[32,2304]{1,0:T(8,128)(2,1)S(1)}, u32[]{:S(2)}, u32[]{:S(2)}) %collective-permute-start.12) | collective-permute-done | bytes 147488 | tf_op jit(solution)/shard_map/ppermute | solution.py:82
  32.7 1.6 %collective-permute-start.3 = (bf16[32,2304]{1,0:T(8,128)(2,1)S(1)}, bf16[32,2304]{1,0:T(8,128)(2,1)S(1)}, u32[]{:S(2)}, u32[]{:S(2)}) collective-permute-start(bf16[32,2304]{1,0:T(8,128)(2,1)S(1)} %collective-permute-done.2), channel_id=1, source_target_pairs={{0,8},{8,16},{16,24},{24,28},{28,20},{20,12},{12,4},{4,0},{1,9},{9... | collective-permute-start | bytes 442376 | tf_op jit(solution)/shard_map/ppermute | solution.py:83
  35.9 1.9 %collective-permute-done.3 = bf16[32,2304]{1,0:T(8,128)(2,1)S(1)} collective-permute-done((bf16[32,2304]{1,0:T(8,128)(2,1)S(1)}, bf16[32,2304]{1,0:T(8,128)(2,1)S(1)}, u32[]{:S(2)}, u32[]{:S(2)}) %collective-permute-start.3) | collective-permute-done | bytes 147488 | tf_op jit(solution)/shard_map/ppermute | solution.py:83
  37.9 1.6 %collective-permute-done.7 = bf16[32,2304]{1,0:T(8,128)(2,1)S(1)} collective-permute-done((bf16[32,2304]{1,0:T(8,128)(2,1)S(1)}, bf16[32,2304]{1,0:T(8,128)(2,1)S(1)}, u32[]{:S(2)}, u32[]{:S(2)}) %collective-permute-start.7) | collective-permute-done | bytes 147488 | tf_op jit(solution)/shard_map/ppermute | solution.py:83
  42.4 1.6 %collective-permute-start.28 = (bf16[32,2304]{1,0:T(8,128)(2,1)S(1)}, bf16[32,2304]{1,0:T(8,128)(2,1)S(1)}, u32[]{:S(2)}, u32[]{:S(2)}) collective-permute-start(bf16[32,2304]{1,0:T(8,128)(2,1)S(1)} %get-tuple-element.29), channel_id=1, source_target_pairs={{0,8},{8,16},{16,24},{24,28},{28,20},{20,12},{12,4},{4,0},{1,9},{9... | collective-permute-start | bytes 442376 | tf_op jit(solution)/shard_map/ppermute | solution.py:123
  51.0 3.5 %collective-permute-start.25 = (bf16[128,2304]{1,0:T(8,128)(2,1)S(1)}, bf16[128,2304]{1,0:T(8,128)(2,1)S(1)}, u32[]{:S(2)}, u32[]{:S(2)}) collective-permute-start(bf16[128,2304]{1,0:T(8,128)(2,1)S(1)} %convolution_convert_fusion), channel_id=1, source_target_pairs={{0,2},{1,3},{4,6},{5,7},{8,10},{9,11},{12,14},{13,15},{16,18},{17,... | collective-permute-start | bytes 1769480 | tf_op jit(solution)/shard_map/ppermute | solution.py:113
  56.3 1.7 %collective-permute-start.36 = (bf16[32,2304]{1,0:T(8,128)(2,1)S(1)}, bf16[32,2304]{1,0:T(8,128)(2,1)S(1)}, u32[]{:S(2)}, u32[]{:S(2)}) collective-permute-start(bf16[32,2304]{1,0:T(8,128)(2,1)S(1)} %get-tuple-element.37), channel_id=1, source_target_pairs={{8,0},{16,8},{24,16},{28,24},{20,28},{12,20},{4,12},{0,4},{9,1},{1... | collective-permute-start | bytes 442376 | tf_op jit(solution)/shard_map/ppermute | solution.py:123
  58.4 1.9 %collective-permute-start.20 = (bf16[32,2304]{1,0:T(8,128)(2,1)S(1)}, bf16[32,2304]{1,0:T(8,128)(2,1)S(1)}, u32[]{:S(2)}, u32[]{:S(2)}) collective-permute-start(bf16[32,2304]{1,0:T(8,128)(2,1)S(1)} %get-tuple-element.42), channel_id=1, source_target_pairs={{8,0},{16,8},{24,16},{28,24},{20,28},{12,20},{4,12},{0,4},{9,1},{1... | collective-permute-start | bytes 442376 | tf_op jit(solution)/shard_map/ppermute | solution.py:123
  60.3 2.4 %collective-permute-done.36 = bf16[32,2304]{1,0:T(8,128)(2,1)S(1)} collective-permute-done((bf16[32,2304]{1,0:T(8,128)(2,1)S(1)}, bf16[32,2304]{1,0:T(8,128)(2,1)S(1)}, u32[]{:S(2)}, u32[]{:S(2)}) %collective-permute-start.36) | collective-permute-done | bytes 147488 | tf_op jit(solution)/shard_map/ppermute | solution.py:123
  65.3 1.6 %collective-permute-start.41 = (bf16[64,2304]{1,0:T(8,128)(2,1)S(1)}, bf16[64,2304]{1,0:T(8,128)(2,1)S(1)}, u32[]{:S(2)}, u32[]{:S(2)}) collective-permute-start(bf16[64,2304]{1,0:T(8,128)(2,1)S(1)} %convolution_convert_fusion.7), channel_id=1, source_target_pairs={{0,2},{1,3},{4,6},{5,7},{8,10},{9,11},{12,14},{13,15},{16,18},{17,... | collective-permute-start | bytes 884744 | tf_op jit(solution)/shard_map/ppermute | solution.py:114
  66.9 1.8 %collective-permute-done.10 = bf16[32,2304]{1,0:T(8,128)(2,1)S(1)} collective-permute-done((bf16[32,2304]{1,0:T(8,128)(2,1)S(1)}, bf16[32,2304]{1,0:T(8,128)(2,1)S(1)}, u32[]{:S(2)}, u32[]{:S(2)}) %collective-permute-start.10) | collective-permute-done | bytes 147488 | tf_op jit(solution)/shard_map/ppermute | solution.py:123
  69.7 4.1 %collective-permute-done.19 = bf16[32,2304]{1,0:T(8,128)(2,1)S(1)} collective-permute-done((bf16[32,2304]{1,0:T(8,128)(2,1)S(1)}, bf16[32,2304]{1,0:T(8,128)(2,1)S(1)}, u32[]{:S(2)}, u32[]{:S(2)}) %collective-permute-start.19) | collective-permute-done | bytes 147488 | tf_op jit(solution)/shard_map/ppermute | solution.py:123
  73.8 1.7 %collective-permute-start.21 = (bf16[32,2304]{1,0:T(8,128)(2,1)S(1)}, bf16[32,2304]{1,0:T(8,128)(2,1)S(1)}, u32[]{:S(2)}, u32[]{:S(2)}) collective-permute-start(bf16[32,2304]{1,0:T(8,128)(2,1)S(1)} %add_convert_fusion.14), channel_id=1, source_target_pairs={{8,0},{16,8},{24,16},{28,24},{20,28},{12,20},{4,12},{0,4},{9,1},{1... | collective-permute-start | bytes 442376 | tf_op jit(solution)/shard_map/ppermute | solution.py:123
  75.6 3.4 %collective-permute-done.21 = bf16[32,2304]{1,0:T(8,128)(2,1)S(1)} collective-permute-done((bf16[32,2304]{1,0:T(8,128)(2,1)S(1)}, bf16[32,2304]{1,0:T(8,128)(2,1)S(1)}, u32[]{:S(2)}, u32[]{:S(2)}) %collective-permute-start.21) | collective-permute-done | bytes 147488 | tf_op jit(solution)/shard_map/ppermute | solution.py:123
  78.9 1.5 %collective-permute-start.30 = (bf16[64,2304]{1,0:T(8,128)(2,1)S(1)}, bf16[64,2304]{1,0:T(8,128)(2,1)S(1)}, u32[]{:S(2)}, u32[]{:S(2)}) collective-permute-start(bf16[64,2304]{1,0:T(8,128)(2,1)S(1)} %pad_maximum_fusion.4), channel_id=1, source_target_pairs={{0,2},{1,3},{4,6},{5,7},{8,10},{9,11},{12,14},{13,15},{16,18},{17,... | collective-permute-start | bytes 884744 | tf_op jit(solution)/shard_map/ppermute | solution.py:131
  80.6 4.1 %collective-permute-done.30 = bf16[64,2304]{1,0:T(8,128)(2,1)S(1)} collective-permute-done((bf16[64,2304]{1,0:T(8,128)(2,1)S(1)}, bf16[64,2304]{1,0:T(8,128)(2,1)S(1)}, u32[]{:S(2)}, u32[]{:S(2)}) %collective-permute-start.30) | collective-permute-done | bytes 294944 | tf_op jit(solution)/shard_map/ppermute | solution.py:131
  84.7 1.7 %collective-permute-start.37 = (bf16[32,2304]{1,0:T(8,128)(2,1)S(1)}, bf16[32,2304]{1,0:T(8,128)(2,1)S(1)}, u32[]{:S(2)}, u32[]{:S(2)}) collective-permute-start(bf16[32,2304]{1,0:T(8,128)(2,1)S(1)} %add_convert_fusion.4), channel_id=1, source_target_pairs={{8,0},{16,8},{24,16},{28,24},{20,28},{12,20},{4,12},{0,4},{9,1},{1... | collective-permute-start | bytes 442376 | tf_op jit(solution)/shard_map/ppermute | solution.py:123
  86.9 4.4 %collective-permute-start.22 = (bf16[64,2304]{1,0:T(8,128)(2,1)S(1)}, bf16[64,2304]{1,0:T(8,128)(2,1)S(1)}, u32[]{:S(2)}, u32[]{:S(2)}) collective-permute-start(bf16[64,2304]{1,0:T(8,128)(2,1)S(1)} %pad_maximum_fusion.3), channel_id=1, source_target_pairs={{0,2},{1,3},{4,6},{5,7},{8,10},{9,11},{12,14},{13,15},{16,18},{17,... | collective-permute-start | bytes 884744 | tf_op jit(solution)/shard_map/ppermute | solution.py:131
  91.4 1.8 %collective-permute-start.34 = (bf16[32,2304]{1,0:T(8,128)(2,1)S(1)}, bf16[32,2304]{1,0:T(8,128)(2,1)S(1)}, u32[]{:S(2)}, u32[]{:S(2)}) collective-permute-start(bf16[32,2304]{1,0:T(8,128)(2,1)S(1)} %add_convert_fusion.6), channel_id=1, source_target_pairs={{8,0},{16,8},{24,16},{28,24},{20,28},{12,20},{4,12},{0,4},{9,1},{1... | collective-permute-start | bytes 442376 | tf_op jit(solution)/shard_map/ppermute | solution.py:123
  93.3 4.7 %collective-permute-done.34 = bf16[32,2304]{1,0:T(8,128)(2,1)S(1)} collective-permute-done((bf16[32,2304]{1,0:T(8,128)(2,1)S(1)}, bf16[32,2304]{1,0:T(8,128)(2,1)S(1)}, u32[]{:S(2)}, u32[]{:S(2)}) %collective-permute-start.34) | collective-permute-done | bytes 147488 | tf_op jit(solution)/shard_map/ppermute | solution.py:123
  100.3 1.8 %collective-permute-start.38 = (bf16[32,2304]{1,0:T(8,128)(2,1)S(1)}, bf16[32,2304]{1,0:T(8,128)(2,1)S(1)}, u32[]{:S(2)}, u32[]{:S(2)}) collective-permute-start(bf16[32,2304]{1,0:T(8,128)(2,1)S(1)} %add_convert_fusion.3), channel_id=1, source_target_pairs={{8,0},{16,8},{24,16},{28,24},{20,28},{12,20},{4,12},{0,4},{9,1},{1... | collective-permute-start | bytes 442376 | tf_op jit(solution)/shard_map/ppermute | solution.py:123
  102.5 1.6 %collective-permute-done.31 = bf16[32,2304]{1,0:T(8,128)(2,1)S(1)} collective-permute-done((bf16[32,2304]{1,0:T(8,128)(2,1)S(1)}, bf16[32,2304]{1,0:T(8,128)(2,1)S(1)}, u32[]{:S(2)}, u32[]{:S(2)}) %collective-permute-start.31) | collective-permute-done | bytes 147488 | tf_op jit(solution)/shard_map/ppermute | solution.py:123
  104.2 1.7 %collective-permute-start.32 = (bf16[32,2304]{1,0:T(8,128)(2,1)S(1)}, bf16[32,2304]{1,0:T(8,128)(2,1)S(1)}, u32[]{:S(2)}, u32[]{:S(2)}) collective-permute-start(bf16[32,2304]{1,0:T(8,128)(2,1)S(1)} %add_convert_fusion.7), channel_id=1, source_target_pairs={{0,8},{8,16},{16,24},{24,28},{28,20},{20,12},{12,4},{4,0},{1,9},{9... | collective-permute-start | bytes 442376 | tf_op jit(solution)/shard_map/ppermute | solution.py:123
  109.7 1.6 %collective-permute-done.39 = bf16[32,2304]{1,0:T(8,128)(2,1)S(1)} collective-permute-done((bf16[32,2304]{1,0:T(8,128)(2,1)S(1)}, bf16[32,2304]{1,0:T(8,128)(2,1)S(1)}, u32[]{:S(2)}, u32[]{:S(2)}) %collective-permute-start.39) | collective-permute-done | bytes 147488 | tf_op jit(solution)/shard_map/ppermute | solution.py:123
  (111 shorter events, 32.3 us)
Async XLA Ops:
  5.0 35.0 %collective-permute-start.9 = (bf16[2,512,2304]{2,1,0:T(8,128)(2,1)S(1)}, bf16[2,512,2304]{2,1,0:T(8,128)(2,1)S(1)}, u32[]{:S(2)}, u32[]{:S(2)}) collective-permute-start(bf16[2,512,2304]{2,1,0:T(8,128)(2,1)S(1)} %pad_maximum_fusion), channel_id=1, source_target_pairs={{0,1},{1,0},{2,3},{3,2},{4,5},{5,4},{6,7},{7,6},{8,9},{9,8},{10,11... | collective-permute-start | bytes 14155784 | tf_op jit(solution)/shard_map/ppermute | solution.py:72
  5.6 10.2 %collective-permute-start = (bf16[64,2304]{1,0:T(8,128)(2,1)S(1)}, bf16[64,2304]{1,0:T(8,128)(2,1)S(1)}, u32[]{:S(2)}, u32[]{:S(2)}) collective-permute-start(bf16[64,2304]{1,0:T(8,128)(2,1)S(1)} %bitcast.69), channel_id=1, source_target_pairs={{0,8},{8,16},{16,24},{24,28},{28,20},{20,12},{12,4},{4,0},{1,9},{9... | collective-permute-start | bytes 884744 | tf_op jit(solution)/shard_map/ppermute | solution.py:77
  8.5 9.1 %collective-permute-start.4 = (bf16[64,2304]{1,0:T(8,128)(2,1)S(1)}, bf16[64,2304]{1,0:T(8,128)(2,1)S(1)}, u32[]{:S(2)}, u32[]{:S(2)}) collective-permute-start(bf16[64,2304]{1,0:T(8,128)(2,1)S(1)} %bitcast.70), channel_id=1, source_target_pairs={{8,0},{16,8},{24,16},{28,24},{20,28},{12,20},{4,12},{0,4},{9,1},{1... | collective-permute-start | bytes 884744 | tf_op jit(solution)/shard_map/ppermute | solution.py:78
  15.8 6.1 %collective-permute-start.1 = (bf16[32,2304]{1,0:T(8,128)(2,1)S(1)}, bf16[32,2304]{1,0:T(8,128)(2,1)S(1)}, u32[]{:S(2)}, u32[]{:S(2)}) collective-permute-start(bf16[32,2304]{1,0:T(8,128)(2,1)S(1)} %get-tuple-element.45), channel_id=1, source_target_pairs={{0,8},{8,16},{16,24},{24,28},{28,20},{20,12},{12,4},{4,0},{1,9},{9... | collective-permute-start | bytes 442376 | tf_op jit(solution)/shard_map/ppermute | solution.py:82
  17.6 6.8 %collective-permute-start.5 = (bf16[32,2304]{1,0:T(8,128)(2,1)S(1)}, bf16[32,2304]{1,0:T(8,128)(2,1)S(1)}, u32[]{:S(2)}, u32[]{:S(2)}) collective-permute-start(bf16[32,2304]{1,0:T(8,128)(2,1)S(1)} %get-tuple-element.44), channel_id=1, source_target_pairs={{8,0},{16,8},{24,16},{28,24},{20,28},{12,20},{4,12},{0,4},{9,1},{1... | collective-permute-start | bytes 442376 | tf_op jit(solution)/shard_map/ppermute | solution.py:82
  17.9 9.7 %collective-permute-start.11 = (bf16[32,2304]{1,0:T(8,128)(2,1)S(1)}, bf16[32,2304]{1,0:T(8,128)(2,1)S(1)}, u32[]{:S(2)}, u32[]{:S(2)}) collective-permute-start(bf16[32,2304]{1,0:T(8,128)(2,1)S(1)} %get-tuple-element.43), channel_id=1, source_target_pairs={{8,0},{16,8},{24,16},{28,24},{20,28},{12,20},{4,12},{0,4},{9,1},{1... | collective-permute-start | bytes 442376 | tf_op jit(solution)/shard_map/ppermute | solution.py:82
  19.7 8.1 %collective-permute-start.13 = (bf16[32,2304]{1,0:T(8,128)(2,1)S(1)}, bf16[32,2304]{1,0:T(8,128)(2,1)S(1)}, u32[]{:S(2)}, u32[]{:S(2)}) collective-permute-start(bf16[32,2304]{1,0:T(8,128)(2,1)S(1)} %get-tuple-element.46), channel_id=1, source_target_pairs={{0,8},{8,16},{16,24},{24,28},{28,20},{20,12},{12,4},{4,0},{1,9},{9... | collective-permute-start | bytes 442376 | tf_op jit(solution)/shard_map/ppermute | solution.py:82
  21.8 8.3 %collective-permute-start.2 = (bf16[32,2304]{1,0:T(8,128)(2,1)S(1)}, bf16[32,2304]{1,0:T(8,128)(2,1)S(1)}, u32[]{:S(2)}, u32[]{:S(2)}) collective-permute-start(bf16[32,2304]{1,0:T(8,128)(2,1)S(1)} %collective-permute-done.1), channel_id=1, source_target_pairs={{0,8},{8,16},{16,24},{24,28},{28,20},{20,12},{12,4},{4,0},{1,9},{9... | collective-permute-start | bytes 442376 | tf_op jit(solution)/shard_map/ppermute | solution.py:82
  24.4 5.9 %collective-permute-start.6 = (bf16[32,2304]{1,0:T(8,128)(2,1)S(1)}, bf16[32,2304]{1,0:T(8,128)(2,1)S(1)}, u32[]{:S(2)}, u32[]{:S(2)}) collective-permute-start(bf16[32,2304]{1,0:T(8,128)(2,1)S(1)} %collective-permute-done.5), channel_id=1, source_target_pairs={{8,0},{16,8},{24,16},{28,24},{20,28},{12,20},{4,12},{0,4},{9,1},{1... | collective-permute-start | bytes 442376 | tf_op jit(solution)/shard_map/ppermute | solution.py:82
  27.8 6.5 %collective-permute-start.14 = (bf16[32,2304]{1,0:T(8,128)(2,1)S(1)}, bf16[32,2304]{1,0:T(8,128)(2,1)S(1)}, u32[]{:S(2)}, u32[]{:S(2)}) collective-permute-start(bf16[32,2304]{1,0:T(8,128)(2,1)S(1)} %collective-permute-done.13), channel_id=1, source_target_pairs={{0,8},{8,16},{16,24},{24,28},{28,20},{20,12},{12,4},{4,0},{1,9},{9... | collective-permute-start | bytes 442376 | tf_op jit(solution)/shard_map/ppermute | solution.py:82
  30.1 24.4 %collective-permute-start.40 = (bf16[64,512]{1,0:T(8,128)(2,1)S(1)}, bf16[64,512]{1,0:T(8,128)(2,1)S(1)}, u32[]{:S(2)}, u32[]{:S(2)}) collective-permute-start(bf16[64,512]{1,0:T(8,128)(2,1)S(1)} %fusion.49), channel_id=1, source_target_pairs={{0,1},{1,0},{2,3},{3,2},{4,5},{5,4},{6,7},{7,6},{8,9},{9,8},{10,11... | collective-permute-start | bytes 196616 | tf_op jit(solution)/shard_map/ppermute | solution.py:90
  30.3 19.9 %collective-permute-start.24 = (bf16[128,512]{1,0:T(8,128)(2,1)S(1)}, bf16[128,512]{1,0:T(8,128)(2,1)S(1)}, u32[]{:S(2)}, u32[]{:S(2)}) collective-permute-start(bf16[128,512]{1,0:T(8,128)(2,1)S(1)} %fusion.34), channel_id=1, source_target_pairs={{0,1},{1,0},{2,3},{3,2},{4,5},{5,4},{6,7},{7,6},{8,9},{9,8},{10,11... | collective-permute-start | bytes 393224 | tf_op jit(solution)/shard_map/ppermute | solution.py:90
  37.9 6.2 %collective-permute-start.17 = (bf16[128,512]{1,0:T(8,128)(2,1)S(1)}, bf16[128,512]{1,0:T(8,128)(2,1)S(1)}, u32[]{:S(2)}, u32[]{:S(2)}) collective-permute-start(bf16[128,512]{1,0:T(8,128)(2,1)S(1)} %fusion.31), channel_id=1, source_target_pairs={{0,1},{1,0},{2,3},{3,2},{4,5},{5,4},{6,7},{7,6},{8,9},{9,8},{10,11... | collective-permute-start | bytes 393224 | tf_op jit(solution)/shard_map/ppermute | solution.py:90
  40.0 7.1 %collective-permute-start.8 = (bf16[64,512]{1,0:T(8,128)(2,1)S(1)}, bf16[64,512]{1,0:T(8,128)(2,1)S(1)}, u32[]{:S(2)}, u32[]{:S(2)}) collective-permute-start(bf16[64,512]{1,0:T(8,128)(2,1)S(1)} %fusion.52), channel_id=1, source_target_pairs={{0,1},{1,0},{2,3},{3,2},{4,5},{5,4},{6,7},{7,6},{8,9},{9,8},{10,11... | collective-permute-start | bytes 196616 | tf_op jit(solution)/shard_map/ppermute | solution.py:90
  42.4 15.6 %collective-permute-start.28 = (bf16[32,2304]{1,0:T(8,128)(2,1)S(1)}, bf16[32,2304]{1,0:T(8,128)(2,1)S(1)}, u32[]{:S(2)}, u32[]{:S(2)}) collective-permute-start(bf16[32,2304]{1,0:T(8,128)(2,1)S(1)} %get-tuple-element.29), channel_id=1, source_target_pairs={{0,8},{8,16},{16,24},{24,28},{28,20},{20,12},{12,4},{4,0},{1,9},{9... | collective-permute-start | bytes 442376 | tf_op jit(solution)/shard_map/ppermute | solution.py:123
  44.9 13.5 %collective-permute-start.29 = (bf16[32,2304]{1,0:T(8,128)(2,1)S(1)}, bf16[32,2304]{1,0:T(8,128)(2,1)S(1)}, u32[]{:S(2)}, u32[]{:S(2)}) collective-permute-start(bf16[32,2304]{1,0:T(8,128)(2,1)S(1)} %get-tuple-element.28), channel_id=1, source_target_pairs={{8,0},{16,8},{24,16},{28,24},{20,28},{12,20},{4,12},{0,4},{9,1},{1... | collective-permute-start | bytes 442376 | tf_op jit(solution)/shard_map/ppermute | solution.py:123
  47.1 39.4 %collective-permute-start.33 = (bf16[32,2304]{1,0:T(8,128)(2,1)S(1)}, bf16[32,2304]{1,0:T(8,128)(2,1)S(1)}, u32[]{:S(2)}, u32[]{:S(2)}) collective-permute-start(bf16[32,2304]{1,0:T(8,128)(2,1)S(1)} %get-tuple-element.15), channel_id=1, source_target_pairs={{8,0},{16,8},{24,16},{28,24},{20,28},{12,20},{4,12},{0,4},{9,1},{1... | collective-permute-start | bytes 442376 | tf_op jit(solution)/shard_map/ppermute | solution.py:123
  51.0 40.3 %collective-permute-start.25 = (bf16[128,2304]{1,0:T(8,128)(2,1)S(1)}, bf16[128,2304]{1,0:T(8,128)(2,1)S(1)}, u32[]{:S(2)}, u32[]{:S(2)}) collective-permute-start(bf16[128,2304]{1,0:T(8,128)(2,1)S(1)} %convolution_convert_fusion), channel_id=1, source_target_pairs={{0,2},{1,3},{4,6},{5,7},{8,10},{9,11},{12,14},{13,15},{16,18},{17,... | collective-permute-start | bytes 1769480 | tf_op jit(solution)/shard_map/ppermute | solution.py:113
  56.3 6.5 %collective-permute-start.36 = (bf16[32,2304]{1,0:T(8,128)(2,1)S(1)}, bf16[32,2304]{1,0:T(8,128)(2,1)S(1)}, u32[]{:S(2)}, u32[]{:S(2)}) collective-permute-start(bf16[32,2304]{1,0:T(8,128)(2,1)S(1)} %get-tuple-element.37), channel_id=1, source_target_pairs={{8,0},{16,8},{24,16},{28,24},{20,28},{12,20},{4,12},{0,4},{9,1},{1... | collective-permute-start | bytes 442376 | tf_op jit(solution)/shard_map/ppermute | solution.py:123
  58.0 6.4 %collective-permute-start.18 = (bf16[32,2304]{1,0:T(8,128)(2,1)S(1)}, bf16[32,2304]{1,0:T(8,128)(2,1)S(1)}, u32[]{:S(2)}, u32[]{:S(2)}) collective-permute-start(bf16[32,2304]{1,0:T(8,128)(2,1)S(1)} %get-tuple-element.41), channel_id=1, source_target_pairs={{0,8},{8,16},{16,24},{24,28},{28,20},{20,12},{12,4},{4,0},{1,9},{9... | collective-permute-start | bytes 442376 | tf_op jit(solution)/shard_map/ppermute | solution.py:123
  58.4 6.9 %collective-permute-start.20 = (bf16[32,2304]{1,0:T(8,128)(2,1)S(1)}, bf16[32,2304]{1,0:T(8,128)(2,1)S(1)}, u32[]{:S(2)}, u32[]{:S(2)}) collective-permute-start(bf16[32,2304]{1,0:T(8,128)(2,1)S(1)} %get-tuple-element.42), channel_id=1, source_target_pairs={{8,0},{16,8},{24,16},{28,24},{20,28},{12,20},{4,12},{0,4},{9,1},{1... | collective-permute-start | bytes 442376 | tf_op jit(solution)/shard_map/ppermute | solution.py:123
  62.7 5.9 %collective-permute-start.10 = (bf16[32,2304]{1,0:T(8,128)(2,1)S(1)}, bf16[32,2304]{1,0:T(8,128)(2,1)S(1)}, u32[]{:S(2)}, u32[]{:S(2)}) collective-permute-start(bf16[32,2304]{1,0:T(8,128)(2,1)S(1)} %get-tuple-element.38), channel_id=1, source_target_pairs={{0,8},{8,16},{16,24},{24,28},{28,20},{20,12},{12,4},{4,0},{1,9},{9... | collective-permute-start | bytes 442376 | tf_op jit(solution)/shard_map/ppermute | solution.py:123
  64.4 22.5 %collective-permute-start.27 = (bf16[32,2304]{1,0:T(8,128)(2,1)S(1)}, bf16[32,2304]{1,0:T(8,128)(2,1)S(1)}, u32[]{:S(2)}, u32[]{:S(2)}) collective-permute-start(bf16[32,2304]{1,0:T(8,128)(2,1)S(1)} %get-tuple-element.17), channel_id=1, source_target_pairs={{0,8},{8,16},{16,24},{24,28},{28,20},{20,12},{12,4},{4,0},{1,9},{9... | collective-permute-start | bytes 442376 | tf_op jit(solution)/shard_map/ppermute | solution.py:123
  65.3 43.9 %collective-permute-start.41 = (bf16[64,2304]{1,0:T(8,128)(2,1)S(1)}, bf16[64,2304]{1,0:T(8,128)(2,1)S(1)}, u32[]{:S(2)}, u32[]{:S(2)}) collective-permute-start(bf16[64,2304]{1,0:T(8,128)(2,1)S(1)} %convolution_convert_fusion.7), channel_id=1, source_target_pairs={{0,2},{1,3},{4,6},{5,7},{8,10},{9,11},{12,14},{13,15},{16,18},{17,... | collective-permute-start | bytes 884744 | tf_op jit(solution)/shard_map/ppermute | solution.py:114
  78.9 5.8 %collective-permute-start.30 = (bf16[64,2304]{1,0:T(8,128)(2,1)S(1)}, bf16[64,2304]{1,0:T(8,128)(2,1)S(1)}, u32[]{:S(2)}, u32[]{:S(2)}) collective-permute-start(bf16[64,2304]{1,0:T(8,128)(2,1)S(1)} %pad_maximum_fusion.4), channel_id=1, source_target_pairs={{0,2},{1,3},{4,6},{5,7},{8,10},{9,11},{12,14},{13,15},{16,18},{17,... | collective-permute-start | bytes 884744 | tf_op jit(solution)/shard_map/ppermute | solution.py:131
  84.7 15.5 %collective-permute-start.37 = (bf16[32,2304]{1,0:T(8,128)(2,1)S(1)}, bf16[32,2304]{1,0:T(8,128)(2,1)S(1)}, u32[]{:S(2)}, u32[]{:S(2)}) collective-permute-start(bf16[32,2304]{1,0:T(8,128)(2,1)S(1)} %add_convert_fusion.4), channel_id=1, source_target_pairs={{8,0},{16,8},{24,16},{28,24},{20,28},{12,20},{4,12},{0,4},{9,1},{1... | collective-permute-start | bytes 442376 | tf_op jit(solution)/shard_map/ppermute | solution.py:123
  86.5 15.6 %collective-permute-start.16 = (bf16[32,2304]{1,0:T(8,128)(2,1)S(1)}, bf16[32,2304]{1,0:T(8,128)(2,1)S(1)}, u32[]{:S(2)}, u32[]{:S(2)}) collective-permute-start(bf16[32,2304]{1,0:T(8,128)(2,1)S(1)} %add_convert_fusion.17), channel_id=1, source_target_pairs={{0,8},{8,16},{16,24},{24,28},{28,20},{20,12},{12,4},{4,0},{1,9},{9... | collective-permute-start | bytes 442376 | tf_op jit(solution)/shard_map/ppermute | solution.py:123
  86.9 12.3 %collective-permute-start.22 = (bf16[64,2304]{1,0:T(8,128)(2,1)S(1)}, bf16[64,2304]{1,0:T(8,128)(2,1)S(1)}, u32[]{:S(2)}, u32[]{:S(2)}) collective-permute-start(bf16[64,2304]{1,0:T(8,128)(2,1)S(1)} %pad_maximum_fusion.3), channel_id=1, source_target_pairs={{0,2},{1,3},{4,6},{5,7},{8,10},{9,11},{12,14},{13,15},{16,18},{17,... | collective-permute-start | bytes 884744 | tf_op jit(solution)/shard_map/ppermute | solution.py:131
  91.4 6.7 %collective-permute-start.34 = (bf16[32,2304]{1,0:T(8,128)(2,1)S(1)}, bf16[32,2304]{1,0:T(8,128)(2,1)S(1)}, u32[]{:S(2)}, u32[]{:S(2)}) collective-permute-start(bf16[32,2304]{1,0:T(8,128)(2,1)S(1)} %add_convert_fusion.6), channel_id=1, source_target_pairs={{8,0},{16,8},{24,16},{28,24},{20,28},{12,20},{4,12},{0,4},{9,1},{1... | collective-permute-start | bytes 442376 | tf_op jit(solution)/shard_map/ppermute | solution.py:123
  98.1 6.1 %collective-permute-start.31 = (bf16[32,2304]{1,0:T(8,128)(2,1)S(1)}, bf16[32,2304]{1,0:T(8,128)(2,1)S(1)}, u32[]{:S(2)}, u32[]{:S(2)}) collective-permute-start(bf16[32,2304]{1,0:T(8,128)(2,1)S(1)} %add_convert_fusion.8), channel_id=1, source_target_pairs={{0,8},{8,16},{16,24},{24,28},{28,20},{20,12},{12,4},{4,0},{1,9},{9... | collective-permute-start | bytes 442376 | tf_op jit(solution)/shard_map/ppermute | solution.py:123
  99.2 9.9 %collective-permute-start.35 = (bf16[32,2304]{1,0:T(8,128)(2,1)S(1)}, bf16[32,2304]{1,0:T(8,128)(2,1)S(1)}, u32[]{:S(2)}, u32[]{:S(2)}) collective-permute-start(bf16[32,2304]{1,0:T(8,128)(2,1)S(1)} %add_convert_fusion.5), channel_id=1, source_target_pairs={{8,0},{16,8},{24,16},{28,24},{20,28},{12,20},{4,12},{0,4},{9,1},{1... | collective-permute-start | bytes 442376 | tf_op jit(solution)/shard_map/ppermute | solution.py:123
  100.3 5.7 %collective-permute-start.38 = (bf16[32,2304]{1,0:T(8,128)(2,1)S(1)}, bf16[32,2304]{1,0:T(8,128)(2,1)S(1)}, u32[]{:S(2)}, u32[]{:S(2)}) collective-permute-start(bf16[32,2304]{1,0:T(8,128)(2,1)S(1)} %add_convert_fusion.3), channel_id=1, source_target_pairs={{8,0},{16,8},{24,16},{28,24},{20,28},{12,20},{4,12},{0,4},{9,1},{1... | collective-permute-start | bytes 442376 | tf_op jit(solution)/shard_map/ppermute | solution.py:123
  (14 other events, 66.6 us)

commit v4 on v3

--- a/solution.py
+++ b/solution.py
@@ -84,14 +84,15 @@
     chunks = [rows] + [jnp.concatenate(bwd[d] + fwd[d], axis=0) for d in range(1, far)] + [jnp.concatenate(ends, axis=0)]
 
     made = []
-    for chunk in chunks:
+    for d, chunk in enumerate(chunks):
         preact = jnp.dot(chunk, enc_weight[0], preferred_element_type=jnp.float32) + enc_bias[0][None, :]
         own = jnp.maximum(preact, 0.0).astype(jnp.bfloat16)
         other = lax.ppermute(own, "layer", swap)
         both = jnp.concatenate([own, other], axis=1)
         pair = []
-        for w in (near, upper):
-            pair.append(jnp.dot(both, w, preferred_element_type=jnp.float32).astype(jnp.bfloat16))
+        for name, w in (("near", near), ("upper", upper)):
+            total = jnp.dot(both, w, preferred_element_type=jnp.float32)
+            pair.append(total if name == "near" and d < far - 1 else total.astype(jnp.bfloat16))
         made.append([lax.optimization_barrier(v) for v in pair])
 
     def piece(which, distance, forward, part):
@@ -112,7 +113,7 @@
 
     got = lax.ppermute(made[1][1], "layer", over)
     straight = lax.ppermute(made[0][1], "layer", over)
-    made[1][0] = lax.optimization_barrier(plus(made[1][0], got))
+    made[1][0] = lax.optimization_barrier(made[1][0] + got.astype(jnp.float32))
 
     crossed = {}
 

time: 114 us -> 114 us (level)
  no operation moved by 1% of the time
where the time goes in v4:
time: 114 us; the launch traced here: 113 us
  starting transfers between devices  50.6 us (44%)
  waiting for transfers between devices  43.3 us (38%)
  matrix products  10.9 us (10%)
  other arithmetic  7.31 us (6%)
    ppermute x20, starting transfers between devices, chain(): got = lax.ppermute(value, 'feat', ahead if forward else back)  23.4 us
    ppermute x20, waiting for transfers between devices, chain(): got = lax.ppermute(value, 'feat', ahead if forward else back)  22.5 us
    ppermute x8, starting transfers between devices, ring_form(): line.append(tuple((lax.ppermute(parts[i], 'feat', pairs) for i in (0, 1))))  8.89 us
    dot_general x10, matrix products, ring_form(): total = jnp.dot(both, w, preferred_element_type=jnp.float32)  8.43 us
    ppermute x1, waiting for transfers between devices, ring_form(): fwd = [(rows,), (lax.ppermute(rows, 'feat', ahead),)]  6.61 us
    ppermute x8, waiting for transfers between devices, ring_form(): line.append(tuple((lax.ppermute(parts[i], 'feat', pairs) for i in (0, 1))))  6.6 us
    ppermute x2, starting transfers between devices, ring_form(): lax.ppermute(jnp.concatenate([chain(1, w, CROSS) for w in pair], axis=0),...  5.93 us
    squeeze x1, other arithmetic, decoder(): return lax.dynamic_index_in_dim(weights[0], target, 0, keepdims=False)  4.52 us
  transfers between devices with their start and end apart: 42, of which 20 were waited for; matrix products, arithmetic and copies ran while one was open for 12% of the time, Pallas kernels for 0%

profile of v4, /device:TPU:0, one launch (start us, length us, event | category | flops | bytes accessed | tf_op | source)
XLA Modules:
  0.0 113.4 jit_solution(788268118148479144)
XLA Ops:
  0.0 4.5 %dynamic-slice_bitcast_fusion = (bf16[512,2304]{1,0:T(8,128)(2,1)S(1)}, bf16[1,512,2304]{2,1,0:T(8,128)(2,1)S(1)}, bf16[512,2304]{1,0:T(8,128)(2,1)S(1)}, bf16[1,512,2304]{2,1,0:T(8,128)(2,1)S(1)}) fusion(bf16[1,4,512,2304]{3,2,1,0:T(8,128)(2,1)} %param.8, s32[]{:T(128)S(6)} %select_n.45, s32[]{:T(128)S(6)} %select_n.41, pred[]{:T(512)S(6)} %eq.5, ...), kind=kLoop, calls=%fused_computation.22 | loop fusion | flops 1179648 | bytes 18874384 | tf_op jit(solution)/shard_map/jit(dynamic_index_in_dim)/squeeze | solution.py:68
  5.6 3.0 %collective-permute-start = (bf16[64,2304]{1,0:T(8,128)(2,1)S(1)}, bf16[64,2304]{1,0:T(8,128)(2,1)S(1)}, u32[]{:S(2)}, u32[]{:S(2)}) collective-permute-start(bf16[64,2304]{1,0:T(8,128)(2,1)S(1)} %bitcast.69), channel_id=1, source_target_pairs={{0,8},{8,16},{16,24},{24,28},{28,20},{20,12},{12,4},{4,0},{1,9},{9... | collective-permute-start | bytes 884744 | tf_op jit(solution)/shard_map/ppermute | solution.py:77
  9.1 6.6 %collective-permute-done = bf16[64,2304]{1,0:T(8,128)(2,1)S(1)} collective-permute-done((bf16[64,2304]{1,0:T(8,128)(2,1)S(1)}, bf16[64,2304]{1,0:T(8,128)(2,1)S(1)}, u32[]{:S(2)}, u32[]{:S(2)}) %collective-permute-start) | collective-permute-done | bytes 294944 | tf_op jit(solution)/shard_map/ppermute | solution.py:77
  15.8 1.9 %collective-permute-start.1 = (bf16[32,2304]{1,0:T(8,128)(2,1)S(1)}, bf16[32,2304]{1,0:T(8,128)(2,1)S(1)}, u32[]{:S(2)}, u32[]{:S(2)}) collective-permute-start(bf16[32,2304]{1,0:T(8,128)(2,1)S(1)} %get-tuple-element.45), channel_id=1, source_target_pairs={{0,8},{8,16},{16,24},{24,28},{28,20},{20,12},{12,4},{4,0},{1,9},{9... | collective-permute-start | bytes 442376 | tf_op jit(solution)/shard_map/ppermute | solution.py:82
  17.9 1.7 %collective-permute-start.11 = (bf16[32,2304]{1,0:T(8,128)(2,1)S(1)}, bf16[32,2304]{1,0:T(8,128)(2,1)S(1)}, u32[]{:S(2)}, u32[]{:S(2)}) collective-permute-start(bf16[32,2304]{1,0:T(8,128)(2,1)S(1)} %get-tuple-element.43), channel_id=1, source_target_pairs={{8,0},{16,8},{24,16},{28,24},{20,28},{12,20},{4,12},{0,4},{9,1},{1... | collective-permute-start | bytes 442376 | tf_op jit(solution)/shard_map/ppermute | solution.py:82
  21.8 2.5 %collective-permute-start.2 = (bf16[32,2304]{1,0:T(8,128)(2,1)S(1)}, bf16[32,2304]{1,0:T(8,128)(2,1)S(1)}, u32[]{:S(2)}, u32[]{:S(2)}) collective-permute-start(bf16[32,2304]{1,0:T(8,128)(2,1)S(1)} %collective-permute-done.1), channel_id=1, source_target_pairs={{0,8},{8,16},{16,24},{24,28},{28,20},{20,12},{12,4},{4,0},{1,9},{9... | collective-permute-start | bytes 442376 | tf_op jit(solution)/shard_map/ppermute | solution.py:82
  24.6 2.9 %collective-permute-done.11 = bf16[32,2304]{1,0:T(8,128)(2,1)S(1)} collective-permute-done((bf16[32,2304]{1,0:T(8,128)(2,1)S(1)}, bf16[32,2304]{1,0:T(8,128)(2,1)S(1)}, u32[]{:S(2)}, u32[]{:S(2)}) %collective-permute-start.11) | collective-permute-done | bytes 147488 | tf_op jit(solution)/shard_map/ppermute | solution.py:82
  27.8 1.8 %collective-permute-start.14 = (bf16[32,2304]{1,0:T(8,128)(2,1)S(1)}, bf16[32,2304]{1,0:T(8,128)(2,1)S(1)}, u32[]{:S(2)}, u32[]{:S(2)}) collective-permute-start(bf16[32,2304]{1,0:T(8,128)(2,1)S(1)} %collective-permute-done.13), channel_id=1, source_target_pairs={{0,8},{8,16},{16,24},{24,28},{28,20},{20,12},{12,4},{4,0},{1,9},{9... | collective-permute-start | bytes 442376 | tf_op jit(solution)/shard_map/ppermute | solution.py:82
  30.7 2.0 %collective-permute-done.12 = bf16[32,2304]{1,0:T(8,128)(2,1)S(1)} collective-permute-done((bf16[32,2304]{1,0:T(8,128)(2,1)S(1)}, bf16[32,2304]{1,0:T(8,128)(2,1)S(1)}, u32[]{:S(2)}, u32[]{:S(2)}) %collective-permute-start.12) | collective-permute-done | bytes 147488 | tf_op jit(solution)/shard_map/ppermute | solution.py:82
  32.7 1.6 %collective-permute-start.3 = (bf16[32,2304]{1,0:T(8,128)(2,1)S(1)}, bf16[32,2304]{1,0:T(8,128)(2,1)S(1)}, u32[]{:S(2)}, u32[]{:S(2)}) collective-permute-start(bf16[32,2304]{1,0:T(8,128)(2,1)S(1)} %collective-permute-done.2), channel_id=1, source_target_pairs={{0,8},{8,16},{16,24},{24,28},{28,20},{20,12},{12,4},{4,0},{1,9},{9... | collective-permute-start | bytes 442376 | tf_op jit(solution)/shard_map/ppermute | solution.py:83
  35.9 1.9 %collective-permute-done.3 = bf16[32,2304]{1,0:T(8,128)(2,1)S(1)} collective-permute-done((bf16[32,2304]{1,0:T(8,128)(2,1)S(1)}, bf16[32,2304]{1,0:T(8,128)(2,1)S(1)}, u32[]{:S(2)}, u32[]{:S(2)}) %collective-permute-start.3) | collective-permute-done | bytes 147488 | tf_op jit(solution)/shard_map/ppermute | solution.py:83
  37.9 1.6 %collective-permute-done.7 = bf16[32,2304]{1,0:T(8,128)(2,1)S(1)} collective-permute-done((bf16[32,2304]{1,0:T(8,128)(2,1)S(1)}, bf16[32,2304]{1,0:T(8,128)(2,1)S(1)}, u32[]{:S(2)}, u32[]{:S(2)}) %collective-permute-start.7) | collective-permute-done | bytes 147488 | tf_op jit(solution)/shard_map/ppermute | solution.py:83
  42.4 1.6 %collective-permute-start.28 = (bf16[32,2304]{1,0:T(8,128)(2,1)S(1)}, bf16[32,2304]{1,0:T(8,128)(2,1)S(1)}, u32[]{:S(2)}, u32[]{:S(2)}) collective-permute-start(bf16[32,2304]{1,0:T(8,128)(2,1)S(1)} %get-tuple-element.29), channel_id=1, source_target_pairs={{0,8},{8,16},{16,24},{24,28},{28,20},{20,12},{12,4},{4,0},{1,9},{9... | collective-permute-start | bytes 442376 | tf_op jit(solution)/shard_map/ppermute | solution.py:124
  51.1 3.5 %collective-permute-start.25 = (bf16[128,2304]{1,0:T(8,128)(2,1)S(1)}, bf16[128,2304]{1,0:T(8,128)(2,1)S(1)}, u32[]{:S(2)}, u32[]{:S(2)}) collective-permute-start(bf16[128,2304]{1,0:T(8,128)(2,1)S(1)} %convolution_convert_fusion), channel_id=1, source_target_pairs={{0,2},{1,3},{4,6},{5,7},{8,10},{9,11},{12,14},{13,15},{16,18},{17,... | collective-permute-start | bytes 1769480 | tf_op jit(solution)/shard_map/ppermute | solution.py:114
  56.3 1.7 %collective-permute-start.36 = (bf16[32,2304]{1,0:T(8,128)(2,1)S(1)}, bf16[32,2304]{1,0:T(8,128)(2,1)S(1)}, u32[]{:S(2)}, u32[]{:S(2)}) collective-permute-start(bf16[32,2304]{1,0:T(8,128)(2,1)S(1)} %get-tuple-element.37), channel_id=1, source_target_pairs={{8,0},{16,8},{24,16},{28,24},{20,28},{12,20},{4,12},{0,4},{9,1},{1... | collective-permute-start | bytes 442376 | tf_op jit(solution)/shard_map/ppermute | solution.py:124
  58.4 1.9 %collective-permute-start.20 = (bf16[32,2304]{1,0:T(8,128)(2,1)S(1)}, bf16[32,2304]{1,0:T(8,128)(2,1)S(1)}, u32[]{:S(2)}, u32[]{:S(2)}) collective-permute-start(bf16[32,2304]{1,0:T(8,128)(2,1)S(1)} %get-tuple-element.42), channel_id=1, source_target_pairs={{8,0},{16,8},{24,16},{28,24},{20,28},{12,20},{4,12},{0,4},{9,1},{1... | collective-permute-start | bytes 442376 | tf_op jit(solution)/shard_map/ppermute | solution.py:124
  60.4 2.4 %collective-permute-done.36 = bf16[32,2304]{1,0:T(8,128)(2,1)S(1)} collective-permute-done((bf16[32,2304]{1,0:T(8,128)(2,1)S(1)}, bf16[32,2304]{1,0:T(8,128)(2,1)S(1)}, u32[]{:S(2)}, u32[]{:S(2)}) %collective-permute-start.36) | collective-permute-done | bytes 147488 | tf_op jit(solution)/shard_map/ppermute | solution.py:124
  65.3 1.6 %collective-permute-start.41 = (bf16[64,2304]{1,0:T(8,128)(2,1)S(1)}, bf16[64,2304]{1,0:T(8,128)(2,1)S(1)}, u32[]{:S(2)}, u32[]{:S(2)}) collective-permute-start(bf16[64,2304]{1,0:T(8,128)(2,1)S(1)} %convolution_convert_fusion.4), channel_id=1, source_target_pairs={{0,2},{1,3},{4,6},{5,7},{8,10},{9,11},{12,14},{13,15},{16,18},{17,... | collective-permute-start | bytes 884744 | tf_op jit(solution)/shard_map/ppermute | solution.py:115
  66.9 1.8 %collective-permute-done.10 = bf16[32,2304]{1,0:T(8,128)(2,1)S(1)} collective-permute-done((bf16[32,2304]{1,0:T(8,128)(2,1)S(1)}, bf16[32,2304]{1,0:T(8,128)(2,1)S(1)}, u32[]{:S(2)}, u32[]{:S(2)}) %collective-permute-start.10) | collective-permute-done | bytes 147488 | tf_op jit(solution)/shard_map/ppermute | solution.py:124
  69.7 4.1 %collective-permute-done.19 = bf16[32,2304]{1,0:T(8,128)(2,1)S(1)} collective-permute-done((bf16[32,2304]{1,0:T(8,128)(2,1)S(1)}, bf16[32,2304]{1,0:T(8,128)(2,1)S(1)}, u32[]{:S(2)}, u32[]{:S(2)}) %collective-permute-start.19) | collective-permute-done | bytes 147488 | tf_op jit(solution)/shard_map/ppermute | solution.py:124
  73.8 1.7 %collective-permute-start.21 = (bf16[32,2304]{1,0:T(8,128)(2,1)S(1)}, bf16[32,2304]{1,0:T(8,128)(2,1)S(1)}, u32[]{:S(2)}, u32[]{:S(2)}) collective-permute-start(bf16[32,2304]{1,0:T(8,128)(2,1)S(1)} %add_convert_fusion.13), channel_id=1, source_target_pairs={{8,0},{16,8},{24,16},{28,24},{20,28},{12,20},{4,12},{0,4},{9,1},{1... | collective-permute-start | bytes 442376 | tf_op jit(solution)/shard_map/ppermute | solution.py:124
  75.6 3.4 %collective-permute-done.21 = bf16[32,2304]{1,0:T(8,128)(2,1)S(1)} collective-permute-done((bf16[32,2304]{1,0:T(8,128)(2,1)S(1)}, bf16[32,2304]{1,0:T(8,128)(2,1)S(1)}, u32[]{:S(2)}, u32[]{:S(2)}) %collective-permute-start.21) | collective-permute-done | bytes 147488 | tf_op jit(solution)/shard_map/ppermute | solution.py:124
  79.0 1.5 %collective-permute-start.30 = (bf16[64,2304]{1,0:T(8,128)(2,1)S(1)}, bf16[64,2304]{1,0:T(8,128)(2,1)S(1)}, u32[]{:S(2)}, u32[]{:S(2)}) collective-permute-start(bf16[64,2304]{1,0:T(8,128)(2,1)S(1)} %pad_maximum_fusion.4), channel_id=1, source_target_pairs={{0,2},{1,3},{4,6},{5,7},{8,10},{9,11},{12,14},{13,15},{16,18},{17,... | collective-permute-start | bytes 884744 | tf_op jit(solution)/shard_map/ppermute | solution.py:132
  80.6 4.1 %collective-permute-done.30 = bf16[64,2304]{1,0:T(8,128)(2,1)S(1)} collective-permute-done((bf16[64,2304]{1,0:T(8,128)(2,1)S(1)}, bf16[64,2304]{1,0:T(8,128)(2,1)S(1)}, u32[]{:S(2)}, u32[]{:S(2)}) %collective-permute-start.30) | collective-permute-done | bytes 294944 | tf_op jit(solution)/shard_map/ppermute | solution.py:132
  84.7 1.7 %collective-permute-start.37 = (bf16[32,2304]{1,0:T(8,128)(2,1)S(1)}, bf16[32,2304]{1,0:T(8,128)(2,1)S(1)}, u32[]{:S(2)}, u32[]{:S(2)}) collective-permute-start(bf16[32,2304]{1,0:T(8,128)(2,1)S(1)} %add_convert_fusion.3), channel_id=1, source_target_pairs={{8,0},{16,8},{24,16},{28,24},{20,28},{12,20},{4,12},{0,4},{9,1},{1... | collective-permute-start | bytes 442376 | tf_op jit(solution)/shard_map/ppermute | solution.py:124
  86.9 4.4 %collective-permute-start.22 = (bf16[64,2304]{1,0:T(8,128)(2,1)S(1)}, bf16[64,2304]{1,0:T(8,128)(2,1)S(1)}, u32[]{:S(2)}, u32[]{:S(2)}) collective-permute-start(bf16[64,2304]{1,0:T(8,128)(2,1)S(1)} %pad_maximum_fusion.3), channel_id=1, source_target_pairs={{0,2},{1,3},{4,6},{5,7},{8,10},{9,11},{12,14},{13,15},{16,18},{17,... | collective-permute-start | bytes 884744 | tf_op jit(solution)/shard_map/ppermute | solution.py:132
  91.4 1.8 %collective-permute-start.34 = (bf16[32,2304]{1,0:T(8,128)(2,1)S(1)}, bf16[32,2304]{1,0:T(8,128)(2,1)S(1)}, u32[]{:S(2)}, u32[]{:S(2)}) collective-permute-start(bf16[32,2304]{1,0:T(8,128)(2,1)S(1)} %add_convert_fusion.5), channel_id=1, source_target_pairs={{8,0},{16,8},{24,16},{28,24},{20,28},{12,20},{4,12},{0,4},{9,1},{1... | collective-permute-start | bytes 442376 | tf_op jit(solution)/shard_map/ppermute | solution.py:124
  93.3 4.7 %collective-permute-done.34 = bf16[32,2304]{1,0:T(8,128)(2,1)S(1)} collective-permute-done((bf16[32,2304]{1,0:T(8,128)(2,1)S(1)}, bf16[32,2304]{1,0:T(8,128)(2,1)S(1)}, u32[]{:S(2)}, u32[]{:S(2)}) %collective-permute-start.34) | collective-permute-done | bytes 147488 | tf_op jit(solution)/shard_map/ppermute | solution.py:124
  100.3 1.8 %collective-permute-start.38 = (bf16[32,2304]{1,0:T(8,128)(2,1)S(1)}, bf16[32,2304]{1,0:T(8,128)(2,1)S(1)}, u32[]{:S(2)}, u32[]{:S(2)}) collective-permute-start(bf16[32,2304]{1,0:T(8,128)(2,1)S(1)} %add_convert_fusion.2), channel_id=1, source_target_pairs={{8,0},{16,8},{24,16},{28,24},{20,28},{12,20},{4,12},{0,4},{9,1},{1... | collective-permute-start | bytes 442376 | tf_op jit(solution)/shard_map/ppermute | solution.py:124
  102.5 1.7 %collective-permute-done.31 = bf16[32,2304]{1,0:T(8,128)(2,1)S(1)} collective-permute-done((bf16[32,2304]{1,0:T(8,128)(2,1)S(1)}, bf16[32,2304]{1,0:T(8,128)(2,1)S(1)}, u32[]{:S(2)}, u32[]{:S(2)}) %collective-permute-start.31) | collective-permute-done | bytes 147488 | tf_op jit(solution)/shard_map/ppermute | solution.py:124
  104.2 1.7 %collective-permute-start.32 = (bf16[32,2304]{1,0:T(8,128)(2,1)S(1)}, bf16[32,2304]{1,0:T(8,128)(2,1)S(1)}, u32[]{:S(2)}, u32[]{:S(2)}) collective-permute-start(bf16[32,2304]{1,0:T(8,128)(2,1)S(1)} %add_convert_fusion.6), channel_id=1, source_target_pairs={{0,8},{8,16},{16,24},{24,28},{28,20},{20,12},{12,4},{4,0},{1,9},{9... | collective-permute-start | bytes 442376 | tf_op jit(solution)/shard_map/ppermute | solution.py:124
  109.7 1.6 %collective-permute-done.39 = bf16[32,2304]{1,0:T(8,128)(2,1)S(1)} collective-permute-done((bf16[32,2304]{1,0:T(8,128)(2,1)S(1)}, bf16[32,2304]{1,0:T(8,128)(2,1)S(1)}, u32[]{:S(2)}, u32[]{:S(2)}) %collective-permute-start.39) | collective-permute-done | bytes 147488 | tf_op jit(solution)/shard_map/ppermute | solution.py:124
  (113 shorter events, 32.3 us)
Async XLA Ops:
  5.0 35.0 %collective-permute-start.9 = (bf16[2,512,2304]{2,1,0:T(8,128)(2,1)S(1)}, bf16[2,512,2304]{2,1,0:T(8,128)(2,1)S(1)}, u32[]{:S(2)}, u32[]{:S(2)}) collective-permute-start(bf16[2,512,2304]{2,1,0:T(8,128)(2,1)S(1)} %pad_maximum_fusion), channel_id=1, source_target_pairs={{0,1},{1,0},{2,3},{3,2},{4,5},{5,4},{6,7},{7,6},{8,9},{9,8},{10,11... | collective-permute-start | bytes 14155784 | tf_op jit(solution)/shard_map/ppermute | solution.py:72
  5.6 10.2 %collective-permute-start = (bf16[64,2304]{1,0:T(8,128)(2,1)S(1)}, bf16[64,2304]{1,0:T(8,128)(2,1)S(1)}, u32[]{:S(2)}, u32[]{:S(2)}) collective-permute-start(bf16[64,2304]{1,0:T(8,128)(2,1)S(1)} %bitcast.69), channel_id=1, source_target_pairs={{0,8},{8,16},{16,24},{24,28},{28,20},{20,12},{12,4},{4,0},{1,9},{9... | collective-permute-start | bytes 884744 | tf_op jit(solution)/shard_map/ppermute | solution.py:77
  8.5 9.1 %collective-permute-start.4 = (bf16[64,2304]{1,0:T(8,128)(2,1)S(1)}, bf16[64,2304]{1,0:T(8,128)(2,1)S(1)}, u32[]{:S(2)}, u32[]{:S(2)}) collective-permute-start(bf16[64,2304]{1,0:T(8,128)(2,1)S(1)} %bitcast.70), channel_id=1, source_target_pairs={{8,0},{16,8},{24,16},{28,24},{20,28},{12,20},{4,12},{0,4},{9,1},{1... | collective-permute-start | bytes 884744 | tf_op jit(solution)/shard_map/ppermute | solution.py:78
  15.8 6.1 %collective-permute-start.1 = (bf16[32,2304]{1,0:T(8,128)(2,1)S(1)}, bf16[32,2304]{1,0:T(8,128)(2,1)S(1)}, u32[]{:S(2)}, u32[]{:S(2)}) collective-permute-start(bf16[32,2304]{1,0:T(8,128)(2,1)S(1)} %get-tuple-element.45), channel_id=1, source_target_pairs={{0,8},{8,16},{16,24},{24,28},{28,20},{20,12},{12,4},{4,0},{1,9},{9... | collective-permute-start | bytes 442376 | tf_op jit(solution)/shard_map/ppermute | solution.py:82
  17.6 6.8 %collective-permute-start.5 = (bf16[32,2304]{1,0:T(8,128)(2,1)S(1)}, bf16[32,2304]{1,0:T(8,128)(2,1)S(1)}, u32[]{:S(2)}, u32[]{:S(2)}) collective-permute-start(bf16[32,2304]{1,0:T(8,128)(2,1)S(1)} %get-tuple-element.44), channel_id=1, source_target_pairs={{8,0},{16,8},{24,16},{28,24},{20,28},{12,20},{4,12},{0,4},{9,1},{1... | collective-permute-start | bytes 442376 | tf_op jit(solution)/shard_map/ppermute | solution.py:82
  17.9 9.7 %collective-permute-start.11 = (bf16[32,2304]{1,0:T(8,128)(2,1)S(1)}, bf16[32,2304]{1,0:T(8,128)(2,1)S(1)}, u32[]{:S(2)}, u32[]{:S(2)}) collective-permute-start(bf16[32,2304]{1,0:T(8,128)(2,1)S(1)} %get-tuple-element.43), channel_id=1, source_target_pairs={{8,0},{16,8},{24,16},{28,24},{20,28},{12,20},{4,12},{0,4},{9,1},{1... | collective-permute-start | bytes 442376 | tf_op jit(solution)/shard_map/ppermute | solution.py:82
  19.7 8.1 %collective-permute-start.13 = (bf16[32,2304]{1,0:T(8,128)(2,1)S(1)}, bf16[32,2304]{1,0:T(8,128)(2,1)S(1)}, u32[]{:S(2)}, u32[]{:S(2)}) collective-permute-start(bf16[32,2304]{1,0:T(8,128)(2,1)S(1)} %get-tuple-element.46), channel_id=1, source_target_pairs={{0,8},{8,16},{16,24},{24,28},{28,20},{20,12},{12,4},{4,0},{1,9},{9... | collective-permute-start | bytes 442376 | tf_op jit(solution)/shard_map/ppermute | solution.py:82
  21.8 8.3 %collective-permute-start.2 = (bf16[32,2304]{1,0:T(8,128)(2,1)S(1)}, bf16[32,2304]{1,0:T(8,128)(2,1)S(1)}, u32[]{:S(2)}, u32[]{:S(2)}) collective-permute-start(bf16[32,2304]{1,0:T(8,128)(2,1)S(1)} %collective-permute-done.1), channel_id=1, source_target_pairs={{0,8},{8,16},{16,24},{24,28},{28,20},{20,12},{12,4},{4,0},{1,9},{9... | collective-permute-start | bytes 442376 | tf_op jit(solution)/shard_map/ppermute | solution.py:82
  24.4 5.9 %collective-permute-start.6 = (bf16[32,2304]{1,0:T(8,128)(2,1)S(1)}, bf16[32,2304]{1,0:T(8,128)(2,1)S(1)}, u32[]{:S(2)}, u32[]{:S(2)}) collective-permute-start(bf16[32,2304]{1,0:T(8,128)(2,1)S(1)} %collective-permute-done.5), channel_id=1, source_target_pairs={{8,0},{16,8},{24,16},{28,24},{20,28},{12,20},{4,12},{0,4},{9,1},{1... | collective-permute-start | bytes 442376 | tf_op jit(solution)/shard_map/ppermute | solution.py:82
  27.8 6.5 %collective-permute-start.14 = (bf16[32,2304]{1,0:T(8,128)(2,1)S(1)}, bf16[32,2304]{1,0:T(8,128)(2,1)S(1)}, u32[]{:S(2)}, u32[]{:S(2)}) collective-permute-start(bf16[32,2304]{1,0:T(8,128)(2,1)S(1)} %collective-permute-done.13), channel_id=1, source_target_pairs={{0,8},{8,16},{16,24},{24,28},{28,20},{20,12},{12,4},{4,0},{1,9},{9... | collective-permute-start | bytes 442376 | tf_op jit(solution)/shard_map/ppermute | solution.py:82
  30.1 24.5 %collective-permute-start.40 = (bf16[64,512]{1,0:T(8,128)(2,1)S(1)}, bf16[64,512]{1,0:T(8,128)(2,1)S(1)}, u32[]{:S(2)}, u32[]{:S(2)}) collective-permute-start(bf16[64,512]{1,0:T(8,128)(2,1)S(1)} %fusion.49), channel_id=1, source_target_pairs={{0,1},{1,0},{2,3},{3,2},{4,5},{5,4},{6,7},{7,6},{8,9},{9,8},{10,11... | collective-permute-start | bytes 196616 | tf_op jit(solution)/shard_map/ppermute | solution.py:90
  30.3 20.0 %collective-permute-start.24 = (bf16[128,512]{1,0:T(8,128)(2,1)S(1)}, bf16[128,512]{1,0:T(8,128)(2,1)S(1)}, u32[]{:S(2)}, u32[]{:S(2)}) collective-permute-start(bf16[128,512]{1,0:T(8,128)(2,1)S(1)} %fusion.34), channel_id=1, source_target_pairs={{0,1},{1,0},{2,3},{3,2},{4,5},{5,4},{6,7},{7,6},{8,9},{9,8},{10,11... | collective-permute-start | bytes 393224 | tf_op jit(solution)/shard_map/ppermute | solution.py:90
  37.9 6.2 %collective-permute-start.17 = (bf16[128,512]{1,0:T(8,128)(2,1)S(1)}, bf16[128,512]{1,0:T(8,128)(2,1)S(1)}, u32[]{:S(2)}, u32[]{:S(2)}) collective-permute-start(bf16[128,512]{1,0:T(8,128)(2,1)S(1)} %fusion.31), channel_id=1, source_target_pairs={{0,1},{1,0},{2,3},{3,2},{4,5},{5,4},{6,7},{7,6},{8,9},{9,8},{10,11... | collective-permute-start | bytes 393224 | tf_op jit(solution)/shard_map/ppermute | solution.py:90
  40.0 7.1 %collective-permute-start.8 = (bf16[64,512]{1,0:T(8,128)(2,1)S(1)}, bf16[64,512]{1,0:T(8,128)(2,1)S(1)}, u32[]{:S(2)}, u32[]{:S(2)}) collective-permute-start(bf16[64,512]{1,0:T(8,128)(2,1)S(1)} %fusion.52), channel_id=1, source_target_pairs={{0,1},{1,0},{2,3},{3,2},{4,5},{5,4},{6,7},{7,6},{8,9},{9,8},{10,11... | collective-permute-start | bytes 196616 | tf_op jit(solution)/shard_map/ppermute | solution.py:90
  42.4 15.6 %collective-permute-start.28 = (bf16[32,2304]{1,0:T(8,128)(2,1)S(1)}, bf16[32,2304]{1,0:T(8,128)(2,1)S(1)}, u32[]{:S(2)}, u32[]{:S(2)}) collective-permute-start(bf16[32,2304]{1,0:T(8,128)(2,1)S(1)} %get-tuple-element.29), channel_id=1, source_target_pairs={{0,8},{8,16},{16,24},{24,28},{28,20},{20,12},{12,4},{4,0},{1,9},{9... | collective-permute-start | bytes 442376 | tf_op jit(solution)/shard_map/ppermute | solution.py:124
  44.9 13.6 %collective-permute-start.29 = (bf16[32,2304]{1,0:T(8,128)(2,1)S(1)}, bf16[32,2304]{1,0:T(8,128)(2,1)S(1)}, u32[]{:S(2)}, u32[]{:S(2)}) collective-permute-start(bf16[32,2304]{1,0:T(8,128)(2,1)S(1)} %get-tuple-element.28), channel_id=1, source_target_pairs={{8,0},{16,8},{24,16},{28,24},{20,28},{12,20},{4,12},{0,4},{9,1},{1... | collective-permute-start | bytes 442376 | tf_op jit(solution)/shard_map/ppermute | solution.py:124
  47.1 39.4 %collective-permute-start.33 = (bf16[32,2304]{1,0:T(8,128)(2,1)S(1)}, bf16[32,2304]{1,0:T(8,128)(2,1)S(1)}, u32[]{:S(2)}, u32[]{:S(2)}) collective-permute-start(bf16[32,2304]{1,0:T(8,128)(2,1)S(1)} %get-tuple-element.23), channel_id=1, source_target_pairs={{8,0},{16,8},{24,16},{28,24},{20,28},{12,20},{4,12},{0,4},{9,1},{1... | collective-permute-start | bytes 442376 | tf_op jit(solution)/shard_map/ppermute | solution.py:124
  51.1 40.3 %collective-permute-start.25 = (bf16[128,2304]{1,0:T(8,128)(2,1)S(1)}, bf16[128,2304]{1,0:T(8,128)(2,1)S(1)}, u32[]{:S(2)}, u32[]{:S(2)}) collective-permute-start(bf16[128,2304]{1,0:T(8,128)(2,1)S(1)} %convolution_convert_fusion), channel_id=1, source_target_pairs={{0,2},{1,3},{4,6},{5,7},{8,10},{9,11},{12,14},{13,15},{16,18},{17,... | collective-permute-start | bytes 1769480 | tf_op jit(solution)/shard_map/ppermute | solution.py:114
  56.3 6.5 %collective-permute-start.36 = (bf16[32,2304]{1,0:T(8,128)(2,1)S(1)}, bf16[32,2304]{1,0:T(8,128)(2,1)S(1)}, u32[]{:S(2)}, u32[]{:S(2)}) collective-permute-start(bf16[32,2304]{1,0:T(8,128)(2,1)S(1)} %get-tuple-element.37), channel_id=1, source_target_pairs={{8,0},{16,8},{24,16},{28,24},{20,28},{12,20},{4,12},{0,4},{9,1},{1... | collective-permute-start | bytes 442376 | tf_op jit(solution)/shard_map/ppermute | solution.py:124
  58.0 6.4 %collective-permute-start.18 = (bf16[32,2304]{1,0:T(8,128)(2,1)S(1)}, bf16[32,2304]{1,0:T(8,128)(2,1)S(1)}, u32[]{:S(2)}, u32[]{:S(2)}) collective-permute-start(bf16[32,2304]{1,0:T(8,128)(2,1)S(1)} %get-tuple-element.41), channel_id=1, source_target_pairs={{0,8},{8,16},{16,24},{24,28},{28,20},{20,12},{12,4},{4,0},{1,9},{9... | collective-permute-start | bytes 442376 | tf_op jit(solution)/shard_map/ppermute | solution.py:124
  58.4 6.9 %collective-permute-start.20 = (bf16[32,2304]{1,0:T(8,128)(2,1)S(1)}, bf16[32,2304]{1,0:T(8,128)(2,1)S(1)}, u32[]{:S(2)}, u32[]{:S(2)}) collective-permute-start(bf16[32,2304]{1,0:T(8,128)(2,1)S(1)} %get-tuple-element.42), channel_id=1, source_target_pairs={{8,0},{16,8},{24,16},{28,24},{20,28},{12,20},{4,12},{0,4},{9,1},{1... | collective-permute-start | bytes 442376 | tf_op jit(solution)/shard_map/ppermute | solution.py:124
  62.8 5.9 %collective-permute-start.10 = (bf16[32,2304]{1,0:T(8,128)(2,1)S(1)}, bf16[32,2304]{1,0:T(8,128)(2,1)S(1)}, u32[]{:S(2)}, u32[]{:S(2)}) collective-permute-start(bf16[32,2304]{1,0:T(8,128)(2,1)S(1)} %get-tuple-element.38), channel_id=1, source_target_pairs={{0,8},{8,16},{16,24},{24,28},{28,20},{20,12},{12,4},{4,0},{1,9},{9... | collective-permute-start | bytes 442376 | tf_op jit(solution)/shard_map/ppermute | solution.py:124
  64.4 22.4 %collective-permute-start.27 = (bf16[32,2304]{1,0:T(8,128)(2,1)S(1)}, bf16[32,2304]{1,0:T(8,128)(2,1)S(1)}, u32[]{:S(2)}, u32[]{:S(2)}) collective-permute-start(bf16[32,2304]{1,0:T(8,128)(2,1)S(1)} %get-tuple-element.25), channel_id=1, source_target_pairs={{0,8},{8,16},{16,24},{24,28},{28,20},{20,12},{12,4},{4,0},{1,9},{9... | collective-permute-start | bytes 442376 | tf_op jit(solution)/shard_map/ppermute | solution.py:124
  65.3 43.8 %collective-permute-start.41 = (bf16[64,2304]{1,0:T(8,128)(2,1)S(1)}, bf16[64,2304]{1,0:T(8,128)(2,1)S(1)}, u32[]{:S(2)}, u32[]{:S(2)}) collective-permute-start(bf16[64,2304]{1,0:T(8,128)(2,1)S(1)} %convolution_convert_fusion.4), channel_id=1, source_target_pairs={{0,2},{1,3},{4,6},{5,7},{8,10},{9,11},{12,14},{13,15},{16,18},{17,... | collective-permute-start | bytes 884744 | tf_op jit(solution)/shard_map/ppermute | solution.py:115
  79.0 5.7 %collective-permute-start.30 = (bf16[64,2304]{1,0:T(8,128)(2,1)S(1)}, bf16[64,2304]{1,0:T(8,128)(2,1)S(1)}, u32[]{:S(2)}, u32[]{:S(2)}) collective-permute-start(bf16[64,2304]{1,0:T(8,128)(2,1)S(1)} %pad_maximum_fusion.4), channel_id=1, source_target_pairs={{0,2},{1,3},{4,6},{5,7},{8,10},{9,11},{12,14},{13,15},{16,18},{17,... | collective-permute-start | bytes 884744 | tf_op jit(solution)/shard_map/ppermute | solution.py:132
  84.7 15.5 %collective-permute-start.37 = (bf16[32,2304]{1,0:T(8,128)(2,1)S(1)}, bf16[32,2304]{1,0:T(8,128)(2,1)S(1)}, u32[]{:S(2)}, u32[]{:S(2)}) collective-permute-start(bf16[32,2304]{1,0:T(8,128)(2,1)S(1)} %add_convert_fusion.3), channel_id=1, source_target_pairs={{8,0},{16,8},{24,16},{28,24},{20,28},{12,20},{4,12},{0,4},{9,1},{1... | collective-permute-start | bytes 442376 | tf_op jit(solution)/shard_map/ppermute | solution.py:124
  86.5 15.6 %collective-permute-start.16 = (bf16[32,2304]{1,0:T(8,128)(2,1)S(1)}, bf16[32,2304]{1,0:T(8,128)(2,1)S(1)}, u32[]{:S(2)}, u32[]{:S(2)}) collective-permute-start(bf16[32,2304]{1,0:T(8,128)(2,1)S(1)} %add_convert_fusion.16), channel_id=1, source_target_pairs={{0,8},{8,16},{16,24},{24,28},{28,20},{20,12},{12,4},{4,0},{1,9},{9... | collective-permute-start | bytes 442376 | tf_op jit(solution)/shard_map/ppermute | solution.py:124
  86.9 12.3 %collective-permute-start.22 = (bf16[64,2304]{1,0:T(8,128)(2,1)S(1)}, bf16[64,2304]{1,0:T(8,128)(2,1)S(1)}, u32[]{:S(2)}, u32[]{:S(2)}) collective-permute-start(bf16[64,2304]{1,0:T(8,128)(2,1)S(1)} %pad_maximum_fusion.3), channel_id=1, source_target_pairs={{0,2},{1,3},{4,6},{5,7},{8,10},{9,11},{12,14},{13,15},{16,18},{17,... | collective-permute-start | bytes 884744 | tf_op jit(solution)/shard_map/ppermute | solution.py:132
  91.4 6.7 %collective-permute-start.34 = (bf16[32,2304]{1,0:T(8,128)(2,1)S(1)}, bf16[32,2304]{1,0:T(8,128)(2,1)S(1)}, u32[]{:S(2)}, u32[]{:S(2)}) collective-permute-start(bf16[32,2304]{1,0:T(8,128)(2,1)S(1)} %add_convert_fusion.5), channel_id=1, source_target_pairs={{8,0},{16,8},{24,16},{28,24},{20,28},{12,20},{4,12},{0,4},{9,1},{1... | collective-permute-start | bytes 442376 | tf_op jit(solution)/shard_map/ppermute | solution.py:124
  98.0 6.1 %collective-permute-start.31 = (bf16[32,2304]{1,0:T(8,128)(2,1)S(1)}, bf16[32,2304]{1,0:T(8,128)(2,1)S(1)}, u32[]{:S(2)}, u32[]{:S(2)}) collective-permute-start(bf16[32,2304]{1,0:T(8,128)(2,1)S(1)} %add_convert_fusion.7), channel_id=1, source_target_pairs={{0,8},{8,16},{16,24},{24,28},{28,20},{20,12},{12,4},{4,0},{1,9},{9... | collective-permute-start | bytes 442376 | tf_op jit(solution)/shard_map/ppermute | solution.py:124
  99.2 9.9 %collective-permute-start.35 = (bf16[32,2304]{1,0:T(8,128)(2,1)S(1)}, bf16[32,2304]{1,0:T(8,128)(2,1)S(1)}, u32[]{:S(2)}, u32[]{:S(2)}) collective-permute-start(bf16[32,2304]{1,0:T(8,128)(2,1)S(1)} %add_convert_fusion.4), channel_id=1, source_target_pairs={{8,0},{16,8},{24,16},{28,24},{20,28},{12,20},{4,12},{0,4},{9,1},{1... | collective-permute-start | bytes 442376 | tf_op jit(solution)/shard_map/ppermute | solution.py:124
  100.3 5.7 %collective-permute-start.38 = (bf16[32,2304]{1,0:T(8,128)(2,1)S(1)}, bf16[32,2304]{1,0:T(8,128)(2,1)S(1)}, u32[]{:S(2)}, u32[]{:S(2)}) collective-permute-start(bf16[32,2304]{1,0:T(8,128)(2,1)S(1)} %add_convert_fusion.2), channel_id=1, source_target_pairs={{8,0},{16,8},{24,16},{28,24},{20,28},{12,20},{4,12},{0,4},{9,1},{1... | collective-permute-start | bytes 442376 | tf_op jit(solution)/shard_map/ppermute | solution.py:124
  (15 other events, 71.8 us)
